TPU v7x, 32 devices: a whole 2x2x4 slice. The times are simulated.
32 devices in a mesh: slab: 4 (over y, x), rcv: 8 (over z, core).
Axes of the slice: x: 2, y: 2, z: 4, core: 2. Of those that a mesh axis runs over, the one named last changes fastest.
Arguments:
- adjoint_now: float32 [8, 16, 128, 128], P('rcv', 'slab'), may hold values from -6 to 6
- adjoint_before: float32 [8, 16, 128, 128], P('rcv', 'slab'), may hold values from -6 to 6
- courant_field: float32 [16, 128, 128], P('slab'), may hold values from 0.04 to 0.2
- log_buoyancy: float32 [16, 128, 128], P('slab'), may hold values from -0.3 to 0.3
- snapshot_store: float32 [8, 16, 128, 128], P('rcv', 'slab'), may hold values from -6 to 6
- owner_order: int32 [8], replicated, may hold values from 0 to 7, each once
- receiver_cells: int32 [8], P('rcv'), may hold values from 0 to 262143
- receiver_traces: float32 [8, 8], P('rcv'), may hold values from -6 to 6
- residual_weights: float32 [8], P('rcv'), may hold values from -0.3 to 0.3
Outputs:
- sensitivity: float32 [16, 128, 128], P('slab', 'rcv')
- adjoint_after: float32 [8, 16, 128, 128], P('rcv', 'slab')
Inputs may be any that keep to these rules, and one draw needn't show every extreme that they name: Each slot number appears once; checkpoint k reads slot owner_order[k] for k < 4. `receiver_cells`: a cell of the grid.
All inputs are finite; a program needn't handle non-finite values.
Results may differ from a plain program's by a relative error of at most 0.0003.
Values sent between devices are 32-bit elements; how exact they have to be, the bound alone decides.
No kernel may reach another device: no remote copies, remote signals or barrier semaphores. Data moves between devices by JAX's collectives and lax.ppermute only.
A program may use at most 64 MiB of HBM per device.

v0:
```python
import functools

import jax
import jax.numpy as jnp
from jax import lax
from jax.experimental import pallas as pl
from jax.experimental.pallas import tpu as pltpu
from jax.sharding import PartitionSpec as P


REACH = (1, -1, 2, -2)
GROUP = 8


VMEM = pl.BlockSpec(memory_space=pltpu.VMEM)
SMEM = pl.BlockSpec(memory_space=pltpu.SMEM)


def swap(block, axis, mask):
    peers = lax.axis_size(axis)
    return lax.ppermute(block, axis, [(i, i ^ mask) for i in range(peers)])


def call(body, outs, inputs, scalars, scratch, flops=0):
    size = sum(x.size * 4 for x in inputs) + sum(4 * functools.reduce(lambda a, b: a * b, o) for o in outs)
    return pl.pallas_call(
        body,
        out_shape=[jax.ShapeDtypeStruct(o, jnp.float32) for o in outs],
        in_specs=[SMEM] * len(scalars) + [VMEM] * len(inputs),
        out_specs=[VMEM] * len(outs),
        scratch_shapes=scratch,
        cost_estimate=pl.CostEstimate(flops=flops, bytes_accessed=size, transcendentals=0),
    )(*scalars, *inputs)


def band(gap, near, far, centre):
    apart = jnp.abs(gap)
    weight = jnp.where(apart == 1, near, jnp.where(apart == 2, far, 0.0))
    if centre is None:
        return jnp.where(gap < 0, -weight, weight)
    return jnp.where(apart == 0, centre, weight)


def fill_bands(lanes, rows):
    size = lanes.shape[0] // 2
    gap = lax.broadcasted_iota(jnp.int32, lanes.shape, 0) % size - lax.broadcasted_iota(jnp.int32, lanes.shape, 1) % size
    column = lax.broadcasted_iota(jnp.int32, lanes.shape, 1)
    lanes[...] = jnp.where(column < size, band(gap, 16.0, -1.0, -90.0), band(gap, 8.0, -1.0, None)).astype(jnp.bfloat16)
    size = rows.shape[0] // 2
    gap = lax.broadcasted_iota(jnp.int32, rows.shape, 1) % size - lax.broadcasted_iota(jnp.int32, rows.shape, 0) % size
    row = lax.broadcasted_iota(jnp.int32, rows.shape, 0)
    rows[...] = jnp.where(row < size, band(gap, 16.0, -1.0, 0.0), band(gap, 8.0, -1.0, None)).astype(jnp.bfloat16)


def differences(ref, x, group, bands):
    lanes, rows = bands
    _, size_z = ref.shape[1:]
    parts = []
    for j in range(group):
        field = ref[x + j]
        high = field.astype(jnp.bfloat16)
        low = (field - high.astype(jnp.float32)).astype(jnp.bfloat16)
        parts.append((high, low))
    flat = jnp.concatenate([jnp.concatenate(p, axis=1) for p in parts], axis=0)
    along_z = jnp.dot(flat, lanes[...], preferred_element_type=jnp.float32)
    along_y = []
    for j in range(0, group, 2):
        pair = jnp.concatenate([jnp.concatenate(p, axis=0) for p in parts[j : j + 2]], axis=1)
        both = jnp.dot(rows[...], pair, preferred_element_type=jnp.float32)
        along_y += [both[:, i * size_z : (i + 1) * size_z] for i in range(2)]
    return along_z, along_y


def prepare(c_ref, b_ref, coef, bands, planes):
    count, size_z = b_ref.shape[1:]
    group = min(GROUP, planes)

    def some(g, carry):
        x = g * group
        along_z, along_y = differences(b_ref, x + 2, group, bands)
        for start in range(0, count, 8):
            rows = slice(start, start + 8)
            stack = [b_ref[x + k, rows, :] for k in range(group + 4)]
            for j in range(group):
                c = c_ref[x + j + 2, rows, :]
                scaled = (1.0 / 144.0) * c
                twelfth = (1.0 / 12.0) * c
                near = 16.0 * twelfth
                p1, m1, p2, m2 = [stack[j + 2 + k] for k in REACH]
                slope = scaled * (8.0 * (p1 - m1) - (p2 - m2))
                steep = 8.0 * slope
                weights = [near + steep, near - steep, -twelfth - slope, slope - twelfth, twelfth]
                weights.append(scaled * along_y[j][count + start : count + start + 8, :])
                weights.append(scaled * along_z[count * j + start : count * j + start + 8, size_z:])
                for i, weight in enumerate(weights):
                    coef[i, x + j, rows, :] = weight
        return carry

    lax.fori_loop(0, planes // group, some, 0)


def advance_planes(cur, old, coef, bands, row_lo, row_hi, x, group):
    count, size_z = cur.shape[1:]
    along_z, along_y = differences(cur, x + 2, group, bands)
    for start in range(row_lo, row_hi, 8):
        rows = slice(start, start + 8)
        stack = [cur[x + k, rows, :] for k in range(group + 4)]
        for j in range(group):
            terms = [coef[i, x + j, rows, :] * stack[j + 2 + k] for i, k in enumerate(REACH)]
            block = along_z[count * j + start : count * j + start + 8, :]
            curved, sloped = along_y[j][rows, :], along_y[j][count + start : count + start + 8, :]
            even = coef[4, x + j, rows, :] * (block[:, :size_z] + curved)
            odd = coef[5, x + j, rows, :] * sloped + coef[6, x + j, rows, :] * block[:, size_z:]
            base = (stack[j + 2] + stack[j + 2]) - old[x + j + 2, rows, :]
            old[x + j + 2, rows, :] = (base + (even + odd)) + ((terms[0] + terms[1]) + (terms[2] + terms[3]))


def advance(cur, old, coef, bands, row_lo, row_hi, total):
    group = min(GROUP, total)
    body = min(2 * group, total)

    def some(g, carry):
        for first in range(0, body, group):
            advance_planes(cur, old, coef, bands, row_lo, row_hi, g * body + first, group)
        return carry

    if body == total:
        some(0, 0)
    else:
        lax.fori_loop(0, total // body, some, 0)


def place(cell, first_row, size_y, size_z):
    return cell // (size_y * size_z), (cell // size_z) % size_y - first_row, cell % size_z


def inject(ref, spot, amplitude):
    x, row, z = spot
    size_z = ref.shape[2]
    base = pl.multiple_of((row // 8) * 8, 8)
    lane = lax.broadcasted_iota(jnp.int32, (8, size_z), 1)
    sub = lax.broadcasted_iota(jnp.int32, (8, size_z), 0)
    hit = (lane == z) & (sub == row - base)
    where = (x + 2, pl.ds(base, 8), slice(None))
    ref[where] = ref[where] + jnp.where(hit, amplitude, 0.0)


def clear_edges(refs, rows):
    for ref in refs:
        planes, count, size_z = ref.shape
        for x in (0, 1, planes - 2, planes - 1):
            ref[x, :, :] = jnp.zeros((count, size_z), jnp.float32)
        if rows < count:
            ref[:, rows:, :] = jnp.zeros((planes, count - rows, size_z), jnp.float32)


def span(step, rows):
    low, high = 2 * (step + 1), rows - 2 * (step + 1)
    return low // 8 * 8, min(rows, -(-high // 8) * 8)


def weigh_body(dims, ids, cells, traces, weights, now, old, own, sent):
    half, size_y, size_z, steps = dims
    core, weight = ids[1], weights[0]
    for i, ref in enumerate((now, old)):
        for j in range(half):
            own[i, j] = weight * ref[half * core + j]
            sent[pl.ds((i * half + j) * size_y, size_y), :] = weight * ref[half * (1 - core) + j]
    lane = lax.broadcasted_iota(jnp.int32, (8, size_z), 1)
    sub = lax.broadcasted_iota(jnp.int32, (8, size_z), 0)
    row = jnp.where(lane == 0, cells[0].astype(jnp.float32), 0.0)
    for step in range(steps):
        row = jnp.where(lane == 1 + step, weight * traces[0, step], row)
    sent[pl.ds(2 * half * size_y, 8), :] = jnp.where(sub == core, row, 0.0)


def pack_body(dims, ids, now, old, courant, logb, *refs):
    slabs, planes, size_y, size_z, share, halo = dims
    outs, wide = refs[:-1], refs[-1]
    window = share + 2 * halo
    half = planes // 2
    slab, core = ids[0], ids[1]
    wide[:, :, 0:halo, :] = jnp.zeros((4, planes, halo, size_z), jnp.float32)
    wide[:, :, halo + size_y :, :] = jnp.zeros((4, planes, halo, size_z), jnp.float32)
    for i, ref in enumerate((courant, logb, now, old)):
        wide[i, :, halo : halo + size_y, :] = ref[...]
    for d in range(slabs):
        first = pl.multiple_of((slab ^ d) * share, 8)
        model, state = outs[2 * d], outs[2 * d + 1]
        for i in range(2):
            if d == 0:
                model[i * planes : (i + 1) * planes] = wide[i, :, pl.ds(first, window), :]
            else:
                model[i * half : (i + 1) * half] = wide[i, pl.ds(half * core, half), pl.ds(first, window), :]
            state[i * planes : (i + 1) * planes] = wide[2 + i, :, pl.ds(first, window), :]


def field_body(dims, ids, cells, traces, *refs):
    slabs, planes, size_y, size_z, share, halo, steps = dims
    window = share + 2 * halo
    half = planes // 2
    total = planes * slabs
    models, states, others = refs[:slabs], refs[slabs : 2 * slabs], refs[2 * slabs : 3 * slabs - 1]
    outs = refs[3 * slabs - 1 : 4 * slabs - 1]
    now, old, c_ref, b_ref, coef, *bands = refs[4 * slabs - 1 :]
    slab, core = ids[0], ids[1]
    clear_edges((now, old, c_ref, b_ref), window)
    fill_bands(*bands)
    inner = slice(0, window)
    for d in range(slabs):
        base = (slab ^ d) * planes + 2
        now[pl.ds(base, planes), inner, :] = states[d][:planes]
        old[pl.ds(base, planes), inner, :] = states[d][planes:]
        for i, ref in enumerate((c_ref, b_ref)):
            if d == 0:
                ref[pl.ds(base, planes), inner, :] = models[0][i * planes : (i + 1) * planes]
            else:
                ref[pl.ds(base + half * core, half), inner, :] = models[d][i * half : (i + 1) * half]
                ref[pl.ds(base + half * (1 - core), half), inner, :] = others[d - 1][i * half : (i + 1) * half]
    prepare(c_ref, b_ref, coef, bands, total)
    spot = place(cells[0], slab * share - halo, size_y, size_z)
    for step in range(steps):
        low, high = span(step, window)
        advance(now, old, coef, bands, low, high, total)

        @pl.when((spot[1] >= 0) & (spot[1] < window))
        def _(target=old, step=step):
            inject(target, spot, traces[0, step])

        now, old = old, now
    for d in range(slabs):
        outs[d][...] = now[pl.ds((slab ^ d) * planes + 2, planes), halo : halo + share, :]


def sub_rows(tile, halo):
    return 2 * halo + (tile if tile % 8 == 0 else 2 * tile)


def sum_body(dims, ids, order, cells, traces, *refs):
    slabs, planes, size_y, size_z, tile, halo, steps, groups = dims
    window = sub_rows(tile, halo)
    half = planes // 2
    total = planes * slabs
    mine, others, snaps = refs[:slabs], refs[slabs : 2 * slabs], refs[2 * slabs]
    out = refs[2 * slabs + 1]
    spots, now, old, c_ref, b_ref, coef, *bands = refs[2 * slabs + 2 :]
    slab, core, chip = ids[0], ids[1], ids[2]
    clear_edges((now, old, c_ref, b_ref), window)
    fill_bands(*bands)
    inner = slice(0, window)
    offset = pl.multiple_of(core * tile, 8) if tile % 8 == 0 else 0
    taken = pl.ds(offset, window)
    for d in range(slabs):
        base = (slab ^ d) * planes + 2
        for i, ref in enumerate((now, old, c_ref, b_ref)):
            ref[pl.ds(base + half * core, half), inner, :] = mine[d][i * half : (i + 1) * half, taken, :]
            ref[pl.ds(base + half * (1 - core), half), inner, :] = others[d][i * half : (i + 1) * half, taken, :]
    prepare(c_ref, b_ref, coef, bands, total)
    first = chip * 2 * tile - halo + offset

    def note(r, found):
        spot = place(cells[r], first, size_y, size_z)
        for i, value in enumerate(spot + (r,)):
            spots[i, found] = value
        return found + ((spot[1] >= 0) & (spot[1] < window)).astype(jnp.int32)

    inside = lax.fori_loop(0, 2 * groups, note, 0)
    acc = jnp.zeros((planes, tile, size_z), jnp.float32)
    for step in range(steps):
        low, high = span(step, window)
        if step == steps - 1:
            advance_planes(now, old, coef, bands, low, high, slab * planes, planes)
        else:
            advance(now, old, coef, bands, low, high, total)

        def add(i, carry, target=old, step=step):
            inject(target, (spots[0, i], spots[1, i], spots[2, i]), traces[spots[3, i], step])
            return carry

        lax.fori_loop(0, inside, add, 0)
        now, old = old, now
        if step % 2 == 1:
            slot = order[step // 2]
            piece = ((slot // 2) ^ chip) * 2 + ((slot % 2) ^ core)
            own = pl.ds(slab * planes + 2, planes)
            top = halo
            field = now[own, top : top + tile, :]
            if tile % 8:
                field = jnp.where(core == 0, field, now[own, top + tile : top + 2 * tile, :])
            acc = acc + field * snaps[piece]
    out[...] = acc


def unpack_body(dims, ids, *refs):
    slabs, share = dims
    out = refs[slabs]
    for d in range(slabs):
        out[:, pl.ds(pl.multiple_of((ids[0] ^ d) * share, 8), share), :] = refs[d][...]


def local(
    adjoint_now,
    adjoint_before,
    courant_field,
    log_buoyancy,
    snapshot_store,
    owner_order,
    receiver_cells,
    receiver_traces,
    residual_weights,
):
    planes, size_y, size_z = courant_field.shape
    steps = receiver_traces.shape[1]
    slabs, ranks = lax.axis_size("slab"), lax.axis_size("rcv")
    chips = ranks // 2
    halo = 2 * steps
    share = size_y // slabs
    tile = size_y // ranks
    half = planes // 2
    window = share + 2 * halo
    wide = 2 * tile + 2 * halo
    total = planes * slabs
    slab = lax.axis_index("slab")
    rank = lax.axis_index("rcv")
    core, chip = rank % 2, rank // 2
    ids = jnp.stack([slab, core, chip]).astype(jnp.int32)
    now, old, store = adjoint_now[0], adjoint_before[0], snapshot_store[0]

    cut = 2 * half * size_y
    own, sent = call(
        functools.partial(weigh_body, (half, size_y, size_z, steps)),
        [(2, half, size_y, size_z), (cut + 8, size_z)],
        [now, old],
        [ids, receiver_cells, receiver_traces, residual_weights],
        [],
    )
    got = swap(sent, "rcv", 1)

    shapes = []
    for d in range(slabs):
        shapes += [((2 * planes if d == 0 else 2 * half), window, size_z), (2 * planes, window, size_z)]
    packed = call(
        functools.partial(pack_body, (slabs, planes, size_y, size_z, share, halo)),
        shapes,
        [now, old, courant_field, log_buoyancy],
        [ids],
        [pltpu.VMEM((4, planes, size_y + 2 * halo, size_z), jnp.float32)],
    )
    models = [packed[0]] + [swap(packed[2 * d], "slab", d) for d in range(1, slabs)]
    states = [packed[1]] + [swap(packed[2 * d + 1], "slab", d) for d in range(1, slabs)]
    others = [swap(models[d], "rcv", 1) for d in range(1, slabs)]

    flat = lambda a: a.reshape(-1, size_z)
    pair = own + got[:cut].reshape(2, half, size_y, size_z)
    pair = jnp.pad(pair, ((0, 0), (0, 0), (halo, halo), (0, 0)))
    info = sent[cut:] + got[cut:]
    received = []
    for d in range(chips):
        rows = lax.dynamic_slice_in_dim(pair, (chip ^ d) * 2 * tile, wide, 2)
        block = jnp.concatenate([flat(rows), info])
        received.append(swap(block, "rcv", 2 * d) if d else block)
    cut = 2 * half * wide
    summed = functools.reduce(jnp.add, [b[:cut] for b in received]).reshape(2 * half, wide, size_z)
    infos = jnp.concatenate([b[cut : cut + 2] for b in received])
    all_cells = infos[:, 0].astype(jnp.int32)
    all_traces = infos[:, 1 : 1 + steps]

    pick = functools.partial(lax.dynamic_index_in_dim, keepdims=False)
    tiles, _ = lax.optimization_barrier((store.reshape(planes, chips, 2, tile, size_z), got))
    tiles = jnp.stack([pick(tiles, core, 2), swap(pick(tiles, 1 - core, 2), "rcv", 1)])
    snaps = [pick(tiles, chip ^ d, 2) for d in range(chips)]
    snaps = jnp.concatenate([snaps[0]] + [swap(snaps[d], "rcv", 2 * d) for d in range(1, chips)])

    model = jnp.stack([courant_field, log_buoyancy])
    model = lax.dynamic_slice_in_dim(model, half * core, half, 1)
    model = jnp.pad(model, ((0, 0), (0, 0), (halo, halo), (0, 0)))
    model = lax.dynamic_slice_in_dim(model, chip * 2 * tile, wide, 2)
    block = jnp.concatenate([summed, model.reshape(2 * half, wide, size_z)])
    mine = [block] + [swap(block, "slab", d) for d in range(1, slabs)]

    def scratch(rows):
        rows = -(-rows // 16) * 16
        return (
            [pltpu.VMEM((total + 4, rows, size_z), jnp.float32)] * 4
            + [pltpu.VMEM((7, total, rows, size_z), jnp.float32)]
            + [pltpu.VMEM((2 * size_z, 2 * size_z), jnp.bfloat16), pltpu.VMEM((2 * rows, 2 * rows), jnp.bfloat16)]
        )

    finals = call(
        functools.partial(field_body, (slabs, planes, size_y, size_z, share, halo, steps)),
        [(planes, share, size_z)] * slabs,
        models + states + others,
        [ids, receiver_cells, receiver_traces],
        scratch(window),
        flops=40 * steps * total * window * size_z,
    )
    mine[1:] = lax.optimization_barrier(tuple(mine[1:]) + tuple(finals))[: slabs - 1]
    back = [finals[0]] + [swap(finals[d], "slab", d) for d in range(1, slabs)]
    theirs = [swap(b, "rcv", 1) for b in mine]
    (sensitivity,) = call(
        functools.partial(sum_body, (slabs, planes, size_y, size_z, tile, halo, steps, chips)),
        [(planes, tile, size_z)],
        mine + theirs + [snaps],
        [ids, owner_order, all_cells, all_traces],
        [pltpu.SMEM((4, 2 * chips + 1), jnp.int32)] + scratch(sub_rows(tile, halo)),
        flops=40 * steps * total * sub_rows(tile, halo) * size_z,
    )
    (after,) = call(functools.partial(unpack_body, (slabs, share)), [(planes, size_y, size_z)], back, [ids], [])
    return (sensitivity, after[None])


def solution(mesh):
    placed = (
        P("rcv", "slab", None, None),
        P("rcv", "slab", None, None),
        P("slab", None, None),
        P("slab", None, None),
        P("rcv", "slab", None, None),
        P(),
        P("rcv"),
        P("rcv", None),
        P("rcv"),
    )

    return jax.shard_map(
        local,
        mesh=mesh,
        in_specs=placed,
        out_specs=(P("slab", "rcv", None), P("rcv", "slab", None, None)),
        check_vma=False,
    )
```

profile of v0, /device:TPU:0, one launch (start us, length us, event | category | flops | bytes accessed | tf_op | source)
XLA Modules:
  0.0 79.2 jit_solution(5904488329305940509)
XLA Ops:
  2.6 1.9 %shard_map.104 = (f32[2,2,128,128]{3,2,1,0:T(8,128)}, f32[520,128]{1,0:T(8,128)}) custom-call(s32[3]{0:T(128)} %pad_add_fusion.ids, s32[1]{0:T(128)S(6)} %copy.19.cells, f32[1,8]{1,0:T(1,128)} %traces.3, f32[1]{0:T(128)S(6)} %copy.20.weights, f32[4,128,128]{2,1,0:T(8,128)} %bitcast.33, f32[4,128,128]{2,1,0:T(8,128)} %bitcast.35), custom_call_target="tpu_custom_call" | custom-call | bytes 1052672 | tf_op jit(solution)/shard_map/pallas_call | solution.py:26
  5.0 2.5 %shard_map.105 = (f32[8,64,128]{2,1,0:T(8,128)}, f32[8,64,128]{2,1,0:T(8,128)}, f32[4,64,128]{2,1,0:T(8,128)}, f32[8,64,128]{2,1,0:T(8,128)}, f32[4,64,128]{2,1,...) custom-call(s32[3]{0:T(128)} %pad_add_fusion.ids, f32[4,128,128]{2,1,0:T(8,128)} %bitcast.34, ...), custom_call_target="tpu_custom_call" | custom-call | bytes 2752512 | tf_op jit(solution)/shard_map/pallas_call | solution.py:26
  7.5 2.5 %collective-permute-start.7 = (f32[4,64,128]{2,1,0:T(8,128)}, f32[4,64,128]{2,1,0:T(8,128)S(1)}, u32[]{:S(2)}, u32[]{:S(2)}) collective-permute-start(f32[4,64,128]{2,1,0:T(8,128)} %get-tuple-element.23), channel_id=1, source_target_pairs={{0,8},{8,0},{16,24},{24,16},{1,9},{9,1},{17,25},{25,17},{2,10},{10... | collective-permute-start | bytes 393224 | tf_op jit(solution)/shard_map/ppermute | solution.py:21
  10.0 1.5 %collective-permute-start.8 = (f32[4,64,128]{2,1,0:T(8,128)}, f32[4,64,128]{2,1,0:T(8,128)S(1)}, u32[]{:S(2)}, u32[]{:S(2)}) collective-permute-start(f32[4,64,128]{2,1,0:T(8,128)} %get-tuple-element.24), channel_id=1, source_target_pairs={{0,16},{8,24},{16,0},{24,8},{1,17},{9,25},{17,1},{25,9},{2,18},{10... | collective-permute-start | bytes 393224 | tf_op jit(solution)/shard_map/ppermute | solution.py:21
  11.6 2.9 %collective-permute-done.7.refs_1_ = f32[4,64,128]{2,1,0:T(8,128)S(1)} collective-permute-done((f32[4,64,128]{2,1,0:T(8,128)}, f32[4,64,128]{2,1,0:T(8,128)S(1)}, u32[]{:S(2)}, u32[]{:S(2)}) %collective-permute-start.7) | collective-permute-done | bytes 131104 | tf_op jit(solution)/shard_map/ppermute | solution.py:21
  16.0 2.1 %collective-permute-start.1 = (f32[264,128]{1,0:T(8,128)S(1)}, f32[264,128]{1,0:T(8,128)S(1)}, u32[]{:S(2)}, u32[]{:S(2)}) collective-permute-start(f32[264,128]{1,0:T(8,128)S(1)} %get-tuple-element.48), channel_id=1, source_target_pairs={{0,2},{1,3},{2,0},{3,1},{4,6},{5,7},{6,4},{7,5},{8,10},{9,11},{10,... | collective-permute-start | bytes 405512 | tf_op jit(solution)/shard_map/ppermute | solution.py:21
  18.1 2.6 %collective-permute-start.2 = (f32[264,128]{1,0:T(8,128)S(1)}, f32[264,128]{1,0:T(8,128)S(1)}, u32[]{:S(2)}, u32[]{:S(2)}) collective-permute-start(f32[264,128]{1,0:T(8,128)S(1)} %get-tuple-element.49), channel_id=1, source_target_pairs={{0,4},{1,5},{2,6},{3,7},{4,0},{5,1},{6,2},{7,3},{8,12},{9,13},{10,... | collective-permute-start | bytes 405512 | tf_op jit(solution)/shard_map/ppermute | solution.py:21
  20.7 1.5 %collective-permute-start.3 = (f32[264,128]{1,0:T(8,128)S(1)}, f32[264,128]{1,0:T(8,128)S(1)}, u32[]{:S(2)}, u32[]{:S(2)}) collective-permute-start(f32[264,128]{1,0:T(8,128)S(1)} %get-tuple-element.50), channel_id=1, source_target_pairs={{0,6},{1,7},{2,4},{3,5},{4,2},{5,3},{6,0},{7,1},{8,14},{9,15},{10,... | collective-permute-start | bytes 405512 | tf_op jit(solution)/shard_map/ppermute | solution.py:21
  23.5 1.8 %collective-permute-start.11 = (f32[8,64,128]{2,1,0:T(8,128)S(1)}, f32[8,64,128]{2,1,0:T(8,128)S(1)}, u32[]{:S(2)}, u32[]{:S(2)}) collective-permute-start(f32[8,64,128]{2,1,0:T(8,128)S(1)} %copy-done.28), channel_id=1, source_target_pairs={{0,16},{8,24},{16,0},{24,8},{1,17},{9,25},{17,1},{25,9},{2,18},{10... | collective-permute-start | bytes 786440 | tf_op jit(solution)/shard_map/ppermute | solution.py:21
  25.3 1.5 %collective-permute-start.12 = (f32[8,64,128]{2,1,0:T(8,128)S(1)}, f32[8,64,128]{2,1,0:T(8,128)S(1)}, u32[]{:S(2)}, u32[]{:S(2)}) collective-permute-start(f32[8,64,128]{2,1,0:T(8,128)S(1)} %copy-done.27), channel_id=1, source_target_pairs={{0,24},{8,16},{16,8},{24,0},{1,25},{9,17},{17,9},{25,1},{2,26},{10... | collective-permute-start | bytes 786440 | tf_op jit(solution)/shard_map/ppermute | solution.py:21
  26.8 4.4 %collective-permute-done.2 = f32[264,128]{1,0:T(8,128)S(1)} collective-permute-done((f32[264,128]{1,0:T(8,128)S(1)}, f32[264,128]{1,0:T(8,128)S(1)}, u32[]{:S(2)}, u32[]{:S(2)}) %collective-permute-start.2) | collective-permute-done | bytes 135200 | tf_op jit(solution)/shard_map/ppermute | solution.py:21
  33.3 1.6 %collective-permute-start.4 = (f32[8,64,128]{2,1,0:T(8,128)S(1)}, f32[8,64,128]{2,1,0:T(8,128)S(1)}, u32[]{:S(2)}, u32[]{:S(2)}) collective-permute-start(f32[8,64,128]{2,1,0:T(8,128)S(1)} %pad_maximum_fusion.refs_0_), channel_id=1, source_target_pairs={{0,8},{8,0},{16,24},{24,16},{1,9},{9,1},{17,25},{25,17},{2,10},{10... | collective-permute-start | bytes 786440 | tf_op jit(solution)/shard_map/ppermute | solution.py:21
  34.9 1.5 %collective-permute-start.5 = (f32[8,64,128]{2,1,0:T(8,128)S(1)}, f32[8,64,128]{2,1,0:T(8,128)S(1)}, u32[]{:S(2)}, u32[]{:S(2)}) collective-permute-start(f32[8,64,128]{2,1,0:T(8,128)S(1)} %pad_maximum_fusion.refs_0_), channel_id=1, source_target_pairs={{0,16},{8,24},{16,0},{24,8},{1,17},{9,25},{17,1},{25,9},{2,18},{10... | collective-permute-start | bytes 786440 | tf_op jit(solution)/shard_map/ppermute | solution.py:21
  36.4 2.5 %collective-permute-start.6 = (f32[8,64,128]{2,1,0:T(8,128)S(1)}, f32[8,64,128]{2,1,0:T(8,128)S(1)}, u32[]{:S(2)}, u32[]{:S(2)}) collective-permute-start(f32[8,64,128]{2,1,0:T(8,128)S(1)} %pad_maximum_fusion.refs_0_), channel_id=1, source_target_pairs={{0,24},{8,16},{16,8},{24,0},{1,25},{9,17},{17,9},{25,1},{2,26},{10... | collective-permute-start | bytes 786440 | tf_op jit(solution)/shard_map/ppermute | solution.py:21
  39.6 6.9 %shard_map.106 = (f32[4,32,128]{2,1,0:T(8,128)}, f32[4,32,128]{2,1,0:T(8,128)}, f32[4,32,128]{2,1,0:T(8,128)}, f32[4,32,128]{2,1,0:T(8,128)}) custom-call(s32[3]{0:T(128)} %pad_add_fusion.ids, s32[1]{0:T(128)S(6)} %copy.19.cells, f32[1,8]{1,0:T(1,128)} %traces.3, f32[8,64,128]{2,1,0:T(8,128)} %get-tuple-element.22.refs_0_, f32[4,64,128]{2,1,0:T(8,128)} %copy-done.15, ...), custom_call_target="tpu_custom_call" | custom-call | flops 41943040 | bytes 2359296 | tf_op jit(solution)/shard_map/pallas_call | solution.py:26
  46.9 4.1 %collective-permute-done.24.refs_1_ = f32[4,32,128]{2,1,0:T(8,128)S(1)} collective-permute-done((f32[4,32,128]{2,1,0:T(8,128)}, f32[4,32,128]{2,1,0:T(8,128)S(1)}, u32[]{:S(2)}, u32[]{:S(2)}) %collective-permute-start.24) | collective-permute-done | bytes 65568 | tf_op jit(solution)/shard_map/ppermute | solution.py:21
  51.2 1.6 %collective-permute-start.26 = (f32[4,32,128]{2,1,0:T(8,128)S(1)}, f32[4,32,128]{2,1,0:T(8,128)S(1)}, u32[]{:S(2)}, u32[]{:S(2)}) collective-permute-start(f32[4,32,128]{2,1,0:T(8,128)S(1)} %copy-done.30), channel_id=1, source_target_pairs={{0,24},{8,16},{16,8},{24,0},{1,25},{9,17},{17,9},{25,1},{2,26},{10... | collective-permute-start | bytes 196616 | tf_op jit(solution)/shard_map/ppermute | solution.py:21
  52.8 2.4 %collective-permute-done.25.refs_2_ = f32[4,32,128]{2,1,0:T(8,128)S(1)} collective-permute-done((f32[4,32,128]{2,1,0:T(8,128)S(1)}, f32[4,32,128]{2,1,0:T(8,128)S(1)}, u32[]{:S(2)}, u32[]{:S(2)}) %collective-permute-start.25) | collective-permute-done | bytes 65568 | tf_op jit(solution)/shard_map/ppermute | solution.py:21
  56.9 1.7 %shard_map.108 = f32[4,128,128]{2,1,0:T(8,128)} custom-call(s32[3]{0:T(128)} %pad_add_fusion.ids, f32[4,32,128]{2,1,0:T(8,128)} %get-tuple-element.30.refs_0_, f32[4,32,128]{2,1,0:T(8,128)} %copy-done.23, f32[4,32,128]{2,1,0:T(8,128)} %copy-done.24, f32[4,32,128]{2,1,0:T(8,128)} %copy-done.25), custom_call_target="tpu_custom_call" | custom-call | bytes 524288 | tf_op jit(solution)/shard_map/pallas_call | solution.py:26
  58.6 1.9 %collective-permute-start.22 = (f32[2,4,16,128]{3,2,1,0:T(8,128)S(1)}, f32[2,4,16,128]{3,2,1,0:T(8,128)S(1)}, u32[]{:S(2)}, u32[]{:S(2)}) collective-permute-start(f32[2,4,16,128]{3,2,1,0:T(8,128)S(1)} %get-tuple-element.40), channel_id=1, source_target_pairs={{0,4},{1,5},{2,6},{3,7},{4,0},{5,1},{6,2},{7,3},{8,12},{9,13},{10,... | collective-permute-start | bytes 196616 | tf_op jit(solution)/shard_map/ppermute | solution.py:21
  62.4 2.1 %collective-permute-done.22 = f32[2,4,16,128]{3,2,1,0:T(8,128)S(1)} collective-permute-done((f32[2,4,16,128]{3,2,1,0:T(8,128)S(1)}, f32[2,4,16,128]{3,2,1,0:T(8,128)S(1)}, u32[]{:S(2)}, u32[]{:S(2)}) %collective-permute-start.22) | collective-permute-done | bytes 65568 | tf_op jit(solution)/shard_map/ppermute | solution.py:21
  64.5 2.5 %collective-permute-start.23 = (f32[2,4,16,128]{3,2,1,0:T(8,128)S(1)}, f32[2,4,16,128]{3,2,1,0:T(8,128)S(1)}, u32[]{:S(2)}, u32[]{:S(2)}) collective-permute-start(f32[2,4,16,128]{3,2,1,0:T(8,128)S(1)} %get-tuple-element.41), channel_id=1, source_target_pairs={{0,6},{1,7},{2,4},{3,5},{4,2},{5,3},{6,0},{7,1},{8,14},{9,15},{10,... | collective-permute-start | bytes 196616 | tf_op jit(solution)/shard_map/ppermute | solution.py:21
  67.6 2.9 %collective-permute-done.23 = f32[2,4,16,128]{3,2,1,0:T(8,128)S(1)} collective-permute-done((f32[2,4,16,128]{3,2,1,0:T(8,128)S(1)}, f32[2,4,16,128]{3,2,1,0:T(8,128)S(1)}, u32[]{:S(2)}, u32[]{:S(2)}) %collective-permute-start.23) | collective-permute-done | bytes 65568 | tf_op jit(solution)/shard_map/ppermute | solution.py:21
  72.9 6.3 %shard_map.107 = f32[4,16,128]{2,1,0:T(8,128)} custom-call(s32[3]{0:T(128)} %pad_add_fusion.ids, s32[8]{0:T(128)} %order.1, s32[8]{0:T(128)} %convert_reduce_fusion.cells, f32[8,8]{1,0:T(8,128)} %slice.44.traces, f32[8,64,128]{2,1,0:T(8,128)} %copy-done, f32[8,64,128]{2,1,0:T(8,128)} %copy-done.3, f32[8,64,128]{2,1,0:T(8,128)} %copy-done.4, ...), custom_call_target="tpu_custom_call" | custom-call | flops 31457280 | bytes 2392064 | tf_op jit(solution)/shard_map/pallas_call | solution.py:26
  (124 shorter events, 13.6 us)
Async XLA Ops:
  4.5 10.0 %collective-permute-start = (f32[520,128]{1,0:T(8,128)}, f32[520,128]{1,0:T(8,128)S(1)}, u32[]{:S(2)}, u32[]{:S(2)}) collective-permute-start(f32[520,128]{1,0:T(8,128)} %get-tuple-element.20), channel_id=1, source_target_pairs={{0,1},{1,0},{2,3},{3,2},{4,5},{5,4},{6,7},{7,6},{8,9},{9,8},{10,11... | collective-permute-start | bytes 798728 | tf_op jit(solution)/shard_map/ppermute | solution.py:21
  7.5 7.0 %collective-permute-start.7 = (f32[4,64,128]{2,1,0:T(8,128)}, f32[4,64,128]{2,1,0:T(8,128)S(1)}, u32[]{:S(2)}, u32[]{:S(2)}) collective-permute-start(f32[4,64,128]{2,1,0:T(8,128)} %get-tuple-element.23), channel_id=1, source_target_pairs={{0,8},{8,0},{16,24},{24,16},{1,9},{9,1},{17,25},{25,17},{2,10},{10... | collective-permute-start | bytes 393224 | tf_op jit(solution)/shard_map/ppermute | solution.py:21
  10.0 10.7 %collective-permute-start.8 = (f32[4,64,128]{2,1,0:T(8,128)}, f32[4,64,128]{2,1,0:T(8,128)S(1)}, u32[]{:S(2)}, u32[]{:S(2)}) collective-permute-start(f32[4,64,128]{2,1,0:T(8,128)} %get-tuple-element.24), channel_id=1, source_target_pairs={{0,16},{8,24},{16,0},{24,8},{1,17},{9,25},{17,1},{25,9},{2,18},{10... | collective-permute-start | bytes 393224 | tf_op jit(solution)/shard_map/ppermute | solution.py:21
  11.5 10.8 %collective-permute-start.9 = (f32[4,64,128]{2,1,0:T(8,128)}, f32[4,64,128]{2,1,0:T(8,128)S(1)}, u32[]{:S(2)}, u32[]{:S(2)}) collective-permute-start(f32[4,64,128]{2,1,0:T(8,128)} %get-tuple-element.25), channel_id=1, source_target_pairs={{0,24},{8,16},{16,8},{24,0},{1,25},{9,17},{17,9},{25,1},{2,26},{10... | collective-permute-start | bytes 393224 | tf_op jit(solution)/shard_map/ppermute | solution.py:21
  14.5 9.0 %collective-permute-start.13 = (f32[4,64,128]{2,1,0:T(8,128)S(1)}, f32[4,64,128]{2,1,0:T(8,128)S(1)}, u32[]{:S(2)}, u32[]{:S(2)}) collective-permute-start(f32[4,64,128]{2,1,0:T(8,128)S(1)} %collective-permute-done.7.refs_1_), channel_id=1, source_target_pairs={{0,1},{1,0},{2,3},{3,2},{4,5},{5,4},{6,7},{7,6},{8,9},{9,8},{10,11... | collective-permute-start | bytes 393224 | tf_op jit(solution)/shard_map/ppermute | solution.py:21
  16.0 9.4 %collective-permute-start.1 = (f32[264,128]{1,0:T(8,128)S(1)}, f32[264,128]{1,0:T(8,128)S(1)}, u32[]{:S(2)}, u32[]{:S(2)}) collective-permute-start(f32[264,128]{1,0:T(8,128)S(1)} %get-tuple-element.48), channel_id=1, source_target_pairs={{0,2},{1,3},{2,0},{3,1},{4,6},{5,7},{6,4},{7,5},{8,10},{9,11},{10,... | collective-permute-start | bytes 405512 | tf_op jit(solution)/shard_map/ppermute | solution.py:21
  18.1 13.1 %collective-permute-start.2 = (f32[264,128]{1,0:T(8,128)S(1)}, f32[264,128]{1,0:T(8,128)S(1)}, u32[]{:S(2)}, u32[]{:S(2)}) collective-permute-start(f32[264,128]{1,0:T(8,128)S(1)} %get-tuple-element.49), channel_id=1, source_target_pairs={{0,4},{1,5},{2,6},{3,7},{4,0},{5,1},{6,2},{7,3},{8,12},{9,13},{10,... | collective-permute-start | bytes 405512 | tf_op jit(solution)/shard_map/ppermute | solution.py:21
  20.7 10.6 %collective-permute-start.3 = (f32[264,128]{1,0:T(8,128)S(1)}, f32[264,128]{1,0:T(8,128)S(1)}, u32[]{:S(2)}, u32[]{:S(2)}) collective-permute-start(f32[264,128]{1,0:T(8,128)S(1)} %get-tuple-element.50), channel_id=1, source_target_pairs={{0,6},{1,7},{2,4},{3,5},{4,2},{5,3},{6,0},{7,1},{8,14},{9,15},{10,... | collective-permute-start | bytes 405512 | tf_op jit(solution)/shard_map/ppermute | solution.py:21
  23.2 11.7 %collective-permute-start.10 = (f32[8,64,128]{2,1,0:T(8,128)S(1)}, f32[8,64,128]{2,1,0:T(8,128)S(1)}, u32[]{:S(2)}, u32[]{:S(2)}) collective-permute-start(f32[8,64,128]{2,1,0:T(8,128)S(1)} %copy-done.29), channel_id=1, source_target_pairs={{0,8},{8,0},{16,24},{24,16},{1,9},{9,1},{17,25},{25,17},{2,10},{10... | collective-permute-start | bytes 786440 | tf_op jit(solution)/shard_map/ppermute | solution.py:21
  23.5 12.9 %collective-permute-start.11 = (f32[8,64,128]{2,1,0:T(8,128)S(1)}, f32[8,64,128]{2,1,0:T(8,128)S(1)}, u32[]{:S(2)}, u32[]{:S(2)}) collective-permute-start(f32[8,64,128]{2,1,0:T(8,128)S(1)} %copy-done.28), channel_id=1, source_target_pairs={{0,16},{8,24},{16,0},{24,8},{1,17},{9,25},{17,1},{25,9},{2,18},{10... | collective-permute-start | bytes 786440 | tf_op jit(solution)/shard_map/ppermute | solution.py:21
  25.3 13.6 %collective-permute-start.12 = (f32[8,64,128]{2,1,0:T(8,128)S(1)}, f32[8,64,128]{2,1,0:T(8,128)S(1)}, u32[]{:S(2)}, u32[]{:S(2)}) collective-permute-start(f32[8,64,128]{2,1,0:T(8,128)S(1)} %copy-done.27), channel_id=1, source_target_pairs={{0,24},{8,16},{16,8},{24,0},{1,25},{9,17},{17,9},{25,1},{2,26},{10... | collective-permute-start | bytes 786440 | tf_op jit(solution)/shard_map/ppermute | solution.py:21
  32.6 18.5 %collective-permute-start.20 = (f32[4,4,16,128]{3,2,0,1:T(8,128)S(1)}, f32[4,4,16,128]{3,2,0,1:T(8,128)S(1)}, u32[]{:S(2)}, u32[]{:S(2)}) collective-permute-start(f32[4,4,16,128]{3,2,0,1:T(8,128)S(1)} %bitcast.47), channel_id=1, source_target_pairs={{0,1},{1,0},{2,3},{3,2},{4,5},{5,4},{6,7},{7,6},{8,9},{9,8},{10,11... | collective-permute-start | bytes 393224 | tf_op jit(solution)/shard_map/ppermute | solution.py:21
  33.3 27.2 %collective-permute-start.4 = (f32[8,64,128]{2,1,0:T(8,128)S(1)}, f32[8,64,128]{2,1,0:T(8,128)S(1)}, u32[]{:S(2)}, u32[]{:S(2)}) collective-permute-start(f32[8,64,128]{2,1,0:T(8,128)S(1)} %pad_maximum_fusion.refs_0_), channel_id=1, source_target_pairs={{0,8},{8,0},{16,24},{24,16},{1,9},{9,1},{17,25},{25,17},{2,10},{10... | collective-permute-start | bytes 786440 | tf_op jit(solution)/shard_map/ppermute | solution.py:21
  34.9 25.7 %collective-permute-start.5 = (f32[8,64,128]{2,1,0:T(8,128)S(1)}, f32[8,64,128]{2,1,0:T(8,128)S(1)}, u32[]{:S(2)}, u32[]{:S(2)}) collective-permute-start(f32[8,64,128]{2,1,0:T(8,128)S(1)} %pad_maximum_fusion.refs_0_), channel_id=1, source_target_pairs={{0,16},{8,24},{16,0},{24,8},{1,17},{9,25},{17,1},{25,9},{2,18},{10... | collective-permute-start | bytes 786440 | tf_op jit(solution)/shard_map/ppermute | solution.py:21
  36.4 24.2 %collective-permute-start.6 = (f32[8,64,128]{2,1,0:T(8,128)S(1)}, f32[8,64,128]{2,1,0:T(8,128)S(1)}, u32[]{:S(2)}, u32[]{:S(2)}) collective-permute-start(f32[8,64,128]{2,1,0:T(8,128)S(1)} %pad_maximum_fusion.refs_0_), channel_id=1, source_target_pairs={{0,24},{8,16},{16,8},{24,0},{1,25},{9,17},{17,9},{25,1},{2,26},{10... | collective-permute-start | bytes 786440 | tf_op jit(solution)/shard_map/ppermute | solution.py:21
  46.5 4.5 %collective-permute-start.24 = (f32[4,32,128]{2,1,0:T(8,128)}, f32[4,32,128]{2,1,0:T(8,128)S(1)}, u32[]{:S(2)}, u32[]{:S(2)}) collective-permute-start(f32[4,32,128]{2,1,0:T(8,128)} %get-tuple-element.31), channel_id=1, source_target_pairs={{0,8},{8,0},{16,24},{24,16},{1,9},{9,1},{17,25},{25,17},{2,10},{10... | collective-permute-start | bytes 196616 | tf_op jit(solution)/shard_map/ppermute | solution.py:21
  51.2 5.2 %collective-permute-start.26 = (f32[4,32,128]{2,1,0:T(8,128)S(1)}, f32[4,32,128]{2,1,0:T(8,128)S(1)}, u32[]{:S(2)}, u32[]{:S(2)}) collective-permute-start(f32[4,32,128]{2,1,0:T(8,128)S(1)} %copy-done.30), channel_id=1, source_target_pairs={{0,24},{8,16},{16,8},{24,0},{1,25},{9,17},{17,9},{25,1},{2,26},{10... | collective-permute-start | bytes 196616 | tf_op jit(solution)/shard_map/ppermute | solution.py:21
  55.3 6.0 %collective-permute-start.21 = (f32[2,4,16,128]{3,2,1,0:T(8,128)S(1)}, f32[2,4,16,128]{3,2,1,0:T(8,128)S(1)}, u32[]{:S(2)}, u32[]{:S(2)}) collective-permute-start(f32[2,4,16,128]{3,2,1,0:T(8,128)S(1)} %get-tuple-element.39), channel_id=1, source_target_pairs={{0,2},{1,3},{2,0},{3,1},{4,6},{5,7},{6,4},{7,5},{8,10},{9,11},{10,... | collective-permute-start | bytes 196616 | tf_op jit(solution)/shard_map/ppermute | solution.py:21
  58.6 5.9 %collective-permute-start.22 = (f32[2,4,16,128]{3,2,1,0:T(8,128)S(1)}, f32[2,4,16,128]{3,2,1,0:T(8,128)S(1)}, u32[]{:S(2)}, u32[]{:S(2)}) collective-permute-start(f32[2,4,16,128]{3,2,1,0:T(8,128)S(1)} %get-tuple-element.40), channel_id=1, source_target_pairs={{0,4},{1,5},{2,6},{3,7},{4,0},{5,1},{6,2},{7,3},{8,12},{9,13},{10,... | collective-permute-start | bytes 196616 | tf_op jit(solution)/shard_map/ppermute | solution.py:21
  60.5 10.7 %collective-permute-start.16 = (f32[8,64,128]{2,1,0:T(8,128)S(1)}, f32[8,64,128]{2,1,0:T(8,128)S(1)}, u32[]{:S(2)}, u32[]{:S(2)}) collective-permute-start(f32[8,64,128]{2,1,0:T(8,128)S(1)} %pad_maximum_fusion.refs_0_), channel_id=1, source_target_pairs={{0,1},{1,0},{2,3},{3,2},{4,5},{5,4},{6,7},{7,6},{8,9},{9,8},{10,11... | collective-permute-start | bytes 786440 | tf_op jit(solution)/shard_map/ppermute | solution.py:21
  60.7 10.6 %collective-permute-start.17 = (f32[8,64,128]{2,1,0:T(8,128)S(1)}, f32[8,64,128]{2,1,0:T(8,128)S(1)}, u32[]{:S(2)}, u32[]{:S(2)}) collective-permute-start(f32[8,64,128]{2,1,0:T(8,128)S(1)} %collective-permute-done.4.refs_1_), channel_id=1, source_target_pairs={{0,1},{1,0},{2,3},{3,2},{4,5},{5,4},{6,7},{7,6},{8,9},{9,8},{10,11... | collective-permute-start | bytes 786440 | tf_op jit(solution)/shard_map/ppermute | solution.py:21
  61.2 10.1 %collective-permute-start.18 = (f32[8,64,128]{2,1,0:T(8,128)S(1)}, f32[8,64,128]{2,1,0:T(8,128)S(1)}, u32[]{:S(2)}, u32[]{:S(2)}) collective-permute-start(f32[8,64,128]{2,1,0:T(8,128)S(1)} %collective-permute-done.5.refs_2_), channel_id=1, source_target_pairs={{0,1},{1,0},{2,3},{3,2},{4,5},{5,4},{6,7},{7,6},{8,9},{9,8},{10,11... | collective-permute-start | bytes 786440 | tf_op jit(solution)/shard_map/ppermute | solution.py:21
  61.3 10.1 %collective-permute-start.19 = (f32[8,64,128]{2,1,0:T(8,128)S(1)}, f32[8,64,128]{2,1,0:T(8,128)S(1)}, u32[]{:S(2)}, u32[]{:S(2)}) collective-permute-start(f32[8,64,128]{2,1,0:T(8,128)S(1)} %collective-permute-done.6.refs_3_), channel_id=1, source_target_pairs={{0,1},{1,0},{2,3},{3,2},{4,5},{5,4},{6,7},{7,6},{8,9},{9,8},{10,11... | collective-permute-start | bytes 786440 | tf_op jit(solution)/shard_map/ppermute | solution.py:21
  64.5 6.1 %collective-permute-start.23 = (f32[2,4,16,128]{3,2,1,0:T(8,128)S(1)}, f32[2,4,16,128]{3,2,1,0:T(8,128)S(1)}, u32[]{:S(2)}, u32[]{:S(2)}) collective-permute-start(f32[2,4,16,128]{3,2,1,0:T(8,128)S(1)} %get-tuple-element.41), channel_id=1, source_target_pairs={{0,6},{1,7},{2,4},{3,5},{4,2},{5,3},{6,0},{7,1},{8,14},{9,15},{10,... | collective-permute-start | bytes 196616 | tf_op jit(solution)/shard_map/ppermute | solution.py:21
  (38 other events, 263.2 us)
where the time goes:
time: 79.5 us; the launch traced here: 79.2 us
  starting transfers between devices  28.4 us (36%)
  waiting for transfers between devices  20.7 us (26%)
  Pallas kernels  19.3 us (24%)
  local copies, waits for them, and re-layouts  5.67 us (7%)
  other arithmetic  2.9 us (4%)
  between operations  2.31 us (3%)
    ppermute x27, starting transfers between devices, swap(): return lax.ppermute(block, axis, [(i, i ^ mask) for i in range(peers)])  28.4 us
    ppermute x27, waiting for transfers between devices, swap(): return lax.ppermute(block, axis, [(i, i ^ mask) for i in range(peers)])  20.7 us
    pallas_call x5, Pallas kernels, call(): pl.pallas_call(body, out_shape=[jax.ShapeDtypeStruct(o, jnp.float32) for...  19.3 us
    unnamed x64, local copies, waits for them, and re-layouts  4.86 us
  transfers between devices with their start and end apart: 27, of which 8 were waited for; matrix products, arithmetic and copies ran while one was open for 4% of the time, Pallas kernels for 14%

commit v1 on v0

--- a/solution.py
+++ b/solution.py
@@ -10,6 +10,7 @@
 
 REACH = (1, -1, 2, -2)
 GROUP = 8
+SPARE = 4 << 20
 
 
 VMEM = pl.BlockSpec(memory_space=pltpu.VMEM)
@@ -21,8 +22,13 @@
     return lax.ppermute(block, axis, [(i, i ^ mask) for i in range(peers)])
 
 
+def count(shape):
+    return functools.reduce(lambda a, b: a * b, shape)
+
+
 def call(body, outs, inputs, scalars, scratch, flops=0):
-    size = sum(x.size * 4 for x in inputs) + sum(4 * functools.reduce(lambda a, b: a * b, o) for o in outs)
+    size = 4 * (sum(x.size for x in inputs) + sum(count(o) for o in outs))
+    held = sum(count(s.shape) * 4 for s in scratch)
     return pl.pallas_call(
         body,
         out_shape=[jax.ShapeDtypeStruct(o, jnp.float32) for o in outs],
@@ -30,7 +36,13 @@
         out_specs=[VMEM] * len(outs),
         scratch_shapes=scratch,
         cost_estimate=pl.CostEstimate(flops=flops, bytes_accessed=size, transcendentals=0),
+        compiler_params=pltpu.CompilerParams(vmem_limit_bytes=size + held + SPARE),
     )(*scalars, *inputs)
+
+
+def position():
+    rank = lax.axis_index("rcv")
+    return lax.axis_index("slab"), rank % 2, rank // 2
 
 
 def band(gap, near, far, centre):
@@ -159,9 +171,13 @@
     return low // 8 * 8, min(rows, -(-high // 8) * 8)
 
 
-def weigh_body(dims, ids, cells, traces, weights, now, old, own, sent):
-    half, size_y, size_z, steps = dims
-    core, weight = ids[1], weights[0]
+def pack_body(dims, cells, traces, weights, now, old, courant, logb, *refs):
+    slabs, planes, size_y, size_z, share, halo, steps = dims
+    own, sent, whole, *outs, wide = refs
+    window = share + 2 * halo
+    half = planes // 2
+    slab, core, _ = position()
+    weight = weights[0]
     for i, ref in enumerate((now, old)):
         for j in range(half):
             own[i, j] = weight * ref[half * core + j]
@@ -172,51 +188,45 @@
     for step in range(steps):
         row = jnp.where(lane == 1 + step, weight * traces[0, step], row)
     sent[pl.ds(2 * half * size_y, 8), :] = jnp.where(sub == core, row, 0.0)
-
-
-def pack_body(dims, ids, now, old, courant, logb, *refs):
-    slabs, planes, size_y, size_z, share, halo = dims
-    outs, wide = refs[:-1], refs[-1]
-    window = share + 2 * halo
-    half = planes // 2
-    slab, core = ids[0], ids[1]
     wide[:, :, 0:halo, :] = jnp.zeros((4, planes, halo, size_z), jnp.float32)
     wide[:, :, halo + size_y :, :] = jnp.zeros((4, planes, halo, size_z), jnp.float32)
     for i, ref in enumerate((courant, logb, now, old)):
         wide[i, :, halo : halo + size_y, :] = ref[...]
     for d in range(slabs):
-        first = pl.multiple_of((slab ^ d) * share, 8)
-        model, state = outs[2 * d], outs[2 * d + 1]
+        rows = pl.ds(pl.multiple_of((slab ^ d) * share, 8), window)
+        if d == 0:
+            for i in range(4):
+                whole[i * planes : (i + 1) * planes] = wide[i, :, rows, :]
+            continue
+        out = outs[d - 1]
         for i in range(2):
-            if d == 0:
-                model[i * planes : (i + 1) * planes] = wide[i, :, pl.ds(first, window), :]
-            else:
-                model[i * half : (i + 1) * half] = wide[i, pl.ds(half * core, half), pl.ds(first, window), :]
-            state[i * planes : (i + 1) * planes] = wide[2 + i, :, pl.ds(first, window), :]
-
-
-def field_body(dims, ids, cells, traces, *refs):
+            out[i * half : (i + 1) * half] = wide[i, pl.ds(half * core, half), rows, :]
+            out[2 * half + i * planes : 2 * half + (i + 1) * planes] = wide[2 + i, :, rows, :]
+
+
+def field_body(dims, cells, traces, whole, *refs):
     slabs, planes, size_y, size_z, share, halo, steps = dims
     window = share + 2 * halo
     half = planes // 2
     total = planes * slabs
-    models, states, others = refs[:slabs], refs[slabs : 2 * slabs], refs[2 * slabs : 3 * slabs - 1]
-    outs = refs[3 * slabs - 1 : 4 * slabs - 1]
-    now, old, c_ref, b_ref, coef, *bands = refs[4 * slabs - 1 :]
-    slab, core = ids[0], ids[1]
+    blocks, others, outs = refs[: slabs - 1], refs[slabs - 1 : 2 * slabs - 2], refs[2 * slabs - 2 : 3 * slabs - 2]
+    now, old, c_ref, b_ref, coef, *bands = refs[3 * slabs - 2 :]
+    slab, core, _ = position()
     clear_edges((now, old, c_ref, b_ref), window)
     fill_bands(*bands)
     inner = slice(0, window)
     for d in range(slabs):
         base = (slab ^ d) * planes + 2
-        now[pl.ds(base, planes), inner, :] = states[d][:planes]
-        old[pl.ds(base, planes), inner, :] = states[d][planes:]
+        if d == 0:
+            for i, ref in enumerate((c_ref, b_ref, now, old)):
+                ref[pl.ds(base, planes), inner, :] = whole[i * planes : (i + 1) * planes]
+            continue
+        for i, ref in enumerate((now, old)):
+            first = 2 * half + i * planes
+            ref[pl.ds(base, planes), inner, :] = blocks[d - 1][first : first + planes]
         for i, ref in enumerate((c_ref, b_ref)):
-            if d == 0:
-                ref[pl.ds(base, planes), inner, :] = models[0][i * planes : (i + 1) * planes]
-            else:
-                ref[pl.ds(base + half * core, half), inner, :] = models[d][i * half : (i + 1) * half]
-                ref[pl.ds(base + half * (1 - core), half), inner, :] = others[d - 1][i * half : (i + 1) * half]
+            ref[pl.ds(base + half * core, half), inner, :] = blocks[d - 1][i * half : (i + 1) * half]
+            ref[pl.ds(base + half * (1 - core), half), inner, :] = others[d - 1][i * half : (i + 1) * half]
     prepare(c_ref, b_ref, coef, bands, total)
     spot = place(cells[0], slab * share - halo, size_y, size_z)
     for step in range(steps):
@@ -236,15 +246,16 @@
     return 2 * halo + (tile if tile % 8 == 0 else 2 * tile)
 
 
-def sum_body(dims, ids, order, cells, traces, *refs):
+def sum_body(dims, order, cells, traces, *refs):
     slabs, planes, size_y, size_z, tile, halo, steps, groups = dims
     window = sub_rows(tile, halo)
     half = planes // 2
     total = planes * slabs
-    mine, others, snaps = refs[:slabs], refs[slabs : 2 * slabs], refs[2 * slabs]
-    out = refs[2 * slabs + 1]
-    spots, now, old, c_ref, b_ref, coef, *bands = refs[2 * slabs + 2 :]
-    slab, core, chip = ids[0], ids[1], ids[2]
+    mine, others, shots = refs[:slabs], refs[slabs : 2 * slabs], refs[2 * slabs : 2 * slabs + groups]
+    out, spots, snaps, now, old, c_ref, b_ref, coef, *bands = refs[2 * slabs + groups :]
+    slab, core, chip = position()
+    for d in range(groups):
+        snaps[2 * d : 2 * d + 2] = shots[d][...]
     clear_edges((now, old, c_ref, b_ref), window)
     fill_bands(*bands)
     inner = slice(0, window)
@@ -291,11 +302,12 @@
     out[...] = acc
 
 
-def unpack_body(dims, ids, *refs):
+def unpack_body(dims, *refs):
     slabs, share = dims
     out = refs[slabs]
+    slab, _, _ = position()
     for d in range(slabs):
-        out[:, pl.ds(pl.multiple_of((ids[0] ^ d) * share, 8), share), :] = refs[d][...]
+        out[:, pl.ds(pl.multiple_of((slab ^ d) * share, 8), share), :] = refs[d][...]
 
 
 def local(
@@ -320,35 +332,22 @@
     window = share + 2 * halo
     wide = 2 * tile + 2 * halo
     total = planes * slabs
-    slab = lax.axis_index("slab")
     rank = lax.axis_index("rcv")
     core, chip = rank % 2, rank // 2
-    ids = jnp.stack([slab, core, chip]).astype(jnp.int32)
     now, old, store = adjoint_now[0], adjoint_before[0], snapshot_store[0]
 
     cut = 2 * half * size_y
-    own, sent = call(
-        functools.partial(weigh_body, (half, size_y, size_z, steps)),
-        [(2, half, size_y, size_z), (cut + 8, size_z)],
-        [now, old],
-        [ids, receiver_cells, receiver_traces, residual_weights],
-        [],
+    own, sent, whole, *blocks = call(
+        functools.partial(pack_body, (slabs, planes, size_y, size_z, share, halo, steps)),
+        [(2, half, size_y, size_z), (cut + 8, size_z), (4 * planes, window, size_z)]
+        + [(2 * half + 2 * planes, window, size_z)] * (slabs - 1),
+        [now, old, courant_field, log_buoyancy],
+        [receiver_cells, receiver_traces, residual_weights],
+        [pltpu.VMEM((4, planes, size_y + 2 * halo, size_z), jnp.float32)],
     )
     got = swap(sent, "rcv", 1)
-
-    shapes = []
-    for d in range(slabs):
-        shapes += [((2 * planes if d == 0 else 2 * half), window, size_z), (2 * planes, window, size_z)]
-    packed = call(
-        functools.partial(pack_body, (slabs, planes, size_y, size_z, share, halo)),
-        shapes,
-        [now, old, courant_field, log_buoyancy],
-        [ids],
-        [pltpu.VMEM((4, planes, size_y + 2 * halo, size_z), jnp.float32)],
-    )
-    models = [packed[0]] + [swap(packed[2 * d], "slab", d) for d in range(1, slabs)]
-    states = [packed[1]] + [swap(packed[2 * d + 1], "slab", d) for d in range(1, slabs)]
-    others = [swap(models[d], "rcv", 1) for d in range(1, slabs)]
+    blocks = [swap(block, "slab", d + 1) for d, block in enumerate(blocks)]
+    others = [swap(block[: 2 * half], "rcv", 1) for block in blocks]
 
     flat = lambda a: a.reshape(-1, size_z)
     pair = own + got[:cut].reshape(2, half, size_y, size_z)
@@ -366,10 +365,10 @@
     all_traces = infos[:, 1 : 1 + steps]
 
     pick = functools.partial(lax.dynamic_index_in_dim, keepdims=False)
-    tiles, _ = lax.optimization_barrier((store.reshape(planes, chips, 2, tile, size_z), got))
+    tiles = store.reshape(planes, chips, 2, tile, size_z)
     tiles = jnp.stack([pick(tiles, core, 2), swap(pick(tiles, 1 - core, 2), "rcv", 1)])
     snaps = [pick(tiles, chip ^ d, 2) for d in range(chips)]
-    snaps = jnp.concatenate([snaps[0]] + [swap(snaps[d], "rcv", 2 * d) for d in range(1, chips)])
+    snaps = [snaps[0]] + [swap(snaps[d], "rcv", 2 * d) for d in range(1, chips)]
 
     model = jnp.stack([courant_field, log_buoyancy])
     model = lax.dynamic_slice_in_dim(model, half * core, half, 1)
@@ -389,8 +388,8 @@
     finals = call(
         functools.partial(field_body, (slabs, planes, size_y, size_z, share, halo, steps)),
         [(planes, share, size_z)] * slabs,
-        models + states + others,
-        [ids, receiver_cells, receiver_traces],
+        [whole] + blocks + others,
+        [receiver_cells, receiver_traces],
         scratch(window),
         flops=40 * steps * total * window * size_z,
     )
@@ -400,12 +399,13 @@
     (sensitivity,) = call(
         functools.partial(sum_body, (slabs, planes, size_y, size_z, tile, halo, steps, chips)),
         [(planes, tile, size_z)],
-        mine + theirs + [snaps],
-        [ids, owner_order, all_cells, all_traces],
-        [pltpu.SMEM((4, 2 * chips + 1), jnp.int32)] + scratch(sub_rows(tile, halo)),
+        mine + theirs + snaps,
+        [owner_order, all_cells, all_traces],
+        [pltpu.SMEM((4, 2 * chips + 1), jnp.int32), pltpu.VMEM((2 * chips, planes, tile, size_z), jnp.float32)]
+        + scratch(sub_rows(tile, halo)),
         flops=40 * steps * total * sub_rows(tile, halo) * size_z,
     )
-    (after,) = call(functools.partial(unpack_body, (slabs, share)), [(planes, size_y, size_z)], back, [ids], [])
+    (after,) = call(functools.partial(unpack_body, (slabs, share)), [(planes, size_y, size_z)], back, [], [])
     return (sensitivity, after[None])
 
 

time: 79.5 us -> 67.7 us (0.85)
  Pallas kernels: 19.3 us -> 12.8 us
  waiting for transfers between devices: 20.7 us -> 16.8 us
  starting transfers between devices: 28.4 us -> 25.9 us
  local copies, waits for them, and re-layouts: 5.67 us -> 7.89 us
  other arithmetic: 2.9 us -> 1.82 us
    pallas_call x5 -> x4, Pallas kernels: 19.3 us -> 12.8 us  [call(): pl.pallas_call(body, out_shape=[jax.ShapeDtypeStruct(o, jnp.float32) for...]
    ppermute x27 -> x24, waiting for transfers between devices: 20.7 us -> 16.8 us  [swap(): return lax.ppermute(block, axis, [(i, i ^ mask) for i in range(peers)])]
    ppermute x27 -> x24, starting transfers between devices: 28.4 us -> 25.9 us  [swap(): return lax.ppermute(block, axis, [(i, i ^ mask) for i in range(peers)])]
    slice x1, local copies, waits for them, and re-layouts: 0.02 us -> 0.97 us  [local(): pair = own + got[:cut].reshape(2, half, size_y, size_z)]
    squeeze x1, other arithmetic: 0.02 us -> 0.85 us  [local(): snaps = [pick(tiles, chip ^ d, 2) for d in range(chips)]]
    unnamed x64 -> x28, local copies, waits for them, and re-layouts: 4.86 us -> 5.4 us
  transfers between devices with their start and end apart: 27 -> 24, of which waited for: 8 -> 6; matrix products, arithmetic and copies ran while one was open for 4% -> 6% of each run, Pallas kernels for 14% -> 9%
where the time goes in v1:
time: 67.7 us; the launch traced here: 67.3 us
  starting transfers between devices  25.9 us (38%)
  waiting for transfers between devices  16.8 us (25%)
  Pallas kernels  12.8 us (19%)
  local copies, waits for them, and re-layouts  7.89 us (12%)
  between operations  2.16 us (3%)
  other arithmetic  1.82 us (3%)
    ppermute x24, starting transfers between devices, swap(): return lax.ppermute(block, axis, [(i, i ^ mask) for i in range(peers)])  25.9 us
    ppermute x24, waiting for transfers between devices, swap(): return lax.ppermute(block, axis, [(i, i ^ mask) for i in range(peers)])  16.8 us
    pallas_call x4, Pallas kernels, call(): pl.pallas_call(body, out_shape=[jax.ShapeDtypeStruct(o, jnp.float32) for...  12.8 us
    unnamed x28, local copies, waits for them, and re-layouts  5.4 us
  transfers between devices with their start and end apart: 24, of which 6 were waited for; matrix products, arithmetic and copies ran while one was open for 6% of the time, Pallas kernels for 9%

profile of v1, /device:TPU:0, one launch (start us, length us, event | category | flops | bytes accessed | tf_op | source)
XLA Modules:
  0.0 67.3 jit_solution(13824406421361066897)
XLA Ops:
  2.6 0.9 %copy-done = f32[4,128,128]{2,1,0:T(8,128)S(1)} copy-done((f32[4,128,128]{2,1,0:T(8,128)S(1)}, f32[4,128,128]{2,1,0:T(8,128)}, u32[]{:S(2)}) %copy-start) | copy-done | bytes 262168
  3.5 0.9 %copy-done.2 = f32[4,128,128]{2,1,0:T(8,128)S(1)} copy-done((f32[4,128,128]{2,1,0:T(8,128)S(1)}, f32[4,128,128]{2,1,0:T(8,128)}, u32[]{:S(2)}) %copy-start.2) | copy-done | bytes 262168
  6.4 1.5 %shard_map.104 = (f32[2,2,128,128]{3,2,1,0:T(8,128)S(1)}, f32[520,128]{1,0:T(8,128)S(1)}, f32[16,64,128]{2,1,0:T(8,128)S(1)}, f32[12,64,128]{2,1,0:T(8,128)S(1)}...) custom-call(s32[1]{0:T(128)S(6)} %copy.19.cells, f32[1,8]{1,0:T(1,128)S(1)} %copy-done.6, f32[1]{0:T(128)S(6)} %copy.20.weights, ...), custom_call_target="tpu_custom_call" | custom-call | bytes 3280896 | tf_op jit(solution)/shard_map/pallas_call | solution.py:32
  8.4 2.5 %collective-permute-start.7 = (f32[12,64,128]{2,1,0:T(8,128)S(1)}, f32[12,64,128]{2,1,0:T(8,128)S(1)}, u32[]{:S(2)}, u32[]{:S(2)}) collective-permute-start(f32[12,64,128]{2,1,0:T(8,128)S(1)} %get-tuple-element.18), channel_id=1, source_target_pairs={{0,8},{8,0},{16,24},{24,16},{1,9},{9,1},{17,25},{25,17},{2,10},{10... | collective-permute-start | bytes 1179656 | tf_op jit(solution)/shard_map/ppermute | solution.py:22
  10.9 1.5 %collective-permute-start.8 = (f32[12,64,128]{2,1,0:T(8,128)}, f32[12,64,128]{2,1,0:T(8,128)S(1)}, u32[]{:S(2)}, u32[]{:S(2)}) collective-permute-start(f32[12,64,128]{2,1,0:T(8,128)} %get-tuple-element.19), channel_id=1, source_target_pairs={{0,16},{8,24},{16,0},{24,8},{1,17},{9,25},{17,1},{25,9},{2,18},{10... | collective-permute-start | bytes 1179656 | tf_op jit(solution)/shard_map/ppermute | solution.py:22
  12.4 1.0 %slice.61 = f32[512,128]{1,0:T(8,128)S(1)} slice(f32[520,128]{1,0:T(8,128)} %collective-permute-done), slice={[0:512], [0:128]} | slice | bytes 524288 | tf_op jit(solution)/shard_map/slice | solution.py:353
  14.2 1.6 %collective-permute-start.1 = (f32[264,128]{1,0:T(8,128)S(1)}, f32[264,128]{1,0:T(8,128)S(1)}, u32[]{:S(2)}, u32[]{:S(2)}) collective-permute-start(f32[264,128]{1,0:T(8,128)S(1)} %get-tuple-element.38), channel_id=1, source_target_pairs={{0,2},{1,3},{2,0},{3,1},{4,6},{5,7},{6,4},{7,5},{8,10},{9,11},{10,... | collective-permute-start | bytes 405512 | tf_op jit(solution)/shard_map/ppermute | solution.py:22
  15.9 2.6 %collective-permute-start.2 = (f32[264,128]{1,0:T(8,128)S(1)}, f32[264,128]{1,0:T(8,128)S(1)}, u32[]{:S(2)}, u32[]{:S(2)}) collective-permute-start(f32[264,128]{1,0:T(8,128)S(1)} %get-tuple-element.39), channel_id=1, source_target_pairs={{0,4},{1,5},{2,6},{3,7},{4,0},{5,1},{6,2},{7,3},{8,12},{9,13},{10,... | collective-permute-start | bytes 405512 | tf_op jit(solution)/shard_map/ppermute | solution.py:22
  19.4 1.3 %collective-permute-done.7.refs_0_ = f32[12,64,128]{2,1,0:T(8,128)S(1)} collective-permute-done((f32[12,64,128]{2,1,0:T(8,128)S(1)}, f32[12,64,128]{2,1,0:T(8,128)S(1)}, u32[]{:S(2)}, u32[]{:S(2)}) %collective-permute-start.7) | collective-permute-done | bytes 393248 | tf_op jit(solution)/shard_map/ppermute | solution.py:22
  20.6 2.7 %collective-permute-start.9 = (f32[12,64,128]{2,1,0:T(8,128)S(1)}, f32[12,64,128]{2,1,0:T(8,128)S(1)}, u32[]{:S(2)}, u32[]{:S(2)}) collective-permute-start(f32[12,64,128]{2,1,0:T(8,128)S(1)} %get-tuple-element.20), channel_id=1, source_target_pairs={{0,24},{8,16},{16,8},{24,0},{1,25},{9,17},{17,9},{25,1},{2,26},{10... | collective-permute-start | bytes 1179656 | tf_op jit(solution)/shard_map/ppermute | solution.py:22
  23.5 5.6 %collective-permute-done.2 = f32[264,128]{1,0:T(8,128)S(1)} collective-permute-done((f32[264,128]{1,0:T(8,128)S(1)}, f32[264,128]{1,0:T(8,128)S(1)}, u32[]{:S(2)}, u32[]{:S(2)}) %collective-permute-start.2) | collective-permute-done | bytes 135200 | tf_op jit(solution)/shard_map/ppermute | solution.py:22
  30.3 1.1 %collective-permute-start.5 = (f32[8,64,128]{2,1,0:T(8,128)S(1)}, f32[8,64,128]{2,1,0:T(8,128)S(1)}, u32[]{:S(2)}, u32[]{:S(2)}) collective-permute-start(f32[8,64,128]{2,1,0:T(8,128)S(1)} %pad_maximum_fusion.refs_0_), channel_id=1, source_target_pairs={{0,16},{8,24},{16,0},{24,8},{1,17},{9,25},{17,1},{25,9},{2,18},{10... | collective-permute-start | bytes 786440 | tf_op jit(solution)/shard_map/ppermute | solution.py:22
  31.4 1.9 %collective-permute-start.6 = (f32[8,64,128]{2,1,0:T(8,128)S(1)}, f32[8,64,128]{2,1,0:T(8,128)S(1)}, u32[]{:S(2)}, u32[]{:S(2)}) collective-permute-start(f32[8,64,128]{2,1,0:T(8,128)S(1)} %pad_maximum_fusion.refs_0_), channel_id=1, source_target_pairs={{0,24},{8,16},{16,8},{24,0},{1,25},{9,17},{17,9},{25,1},{2,26},{10... | collective-permute-start | bytes 786440 | tf_op jit(solution)/shard_map/ppermute | solution.py:22
  35.8 2.2 %collective-permute-start.18 = (f32[2,4,16,128]{3,2,1,0:T(8,128)S(1)}, f32[2,4,16,128]{3,2,1,0:T(8,128)S(1)}, u32[]{:S(2)}, u32[]{:S(2)}) collective-permute-start(f32[2,4,16,128]{3,2,1,0:T(8,128)S(1)} %get-tuple-element.30), channel_id=1, source_target_pairs={{0,2},{1,3},{2,0},{3,1},{4,6},{5,7},{6,4},{7,5},{8,10},{9,11},{10,... | collective-permute-start | bytes 196616 | tf_op jit(solution)/shard_map/ppermute | solution.py:22
  38.0 1.4 %collective-permute-start.19 = (f32[2,4,16,128]{3,2,1,0:T(8,128)S(1)}, f32[2,4,16,128]{3,2,1,0:T(8,128)S(1)}, u32[]{:S(2)}, u32[]{:S(2)}) collective-permute-start(f32[2,4,16,128]{3,2,1,0:T(8,128)S(1)} %get-tuple-element.31), channel_id=1, source_target_pairs={{0,4},{1,5},{2,6},{3,7},{4,0},{5,1},{6,2},{7,3},{8,12},{9,13},{10,... | collective-permute-start | bytes 196616 | tf_op jit(solution)/shard_map/ppermute | solution.py:22
  39.4 5.2 %shard_map.105 = (f32[4,32,128]{2,1,0:T(8,128)S(1)}, f32[4,32,128]{2,1,0:T(8,128)S(1)}, f32[4,32,128]{2,1,0:T(8,128)S(1)}, f32[4,32,128]{2,1,0:T(8,128)S(1)}) custom-call(s32[1]{0:T(128)S(6)} %copy.19.cells, f32[1,8]{1,0:T(1,128)S(1)} %copy-done.6, f32[16,64,128]{2,1,0:T(8,128)S(1)} %get-tuple-element.17.whole, ...), custom_call_target="tpu_custom_call" | custom-call | flops 41943040 | bytes 2359296 | tf_op jit(solution)/shard_map/pallas_call | solution.py:32
  44.6 1.8 %collective-permute-start.21 = (f32[4,32,128]{2,1,0:T(8,128)S(1)}, f32[4,32,128]{2,1,0:T(8,128)S(1)}, u32[]{:S(2)}, u32[]{:S(2)}) collective-permute-start(f32[4,32,128]{2,1,0:T(8,128)S(1)} %get-tuple-element.22), channel_id=1, source_target_pairs={{0,8},{8,0},{16,24},{24,16},{1,9},{9,1},{17,25},{25,17},{2,10},{10... | collective-permute-start | bytes 196616 | tf_op jit(solution)/shard_map/ppermute | solution.py:22
  46.4 1.6 %collective-permute-start.22 = (f32[4,32,128]{2,1,0:T(8,128)S(1)}, f32[4,32,128]{2,1,0:T(8,128)S(1)}, u32[]{:S(2)}, u32[]{:S(2)}) collective-permute-start(f32[4,32,128]{2,1,0:T(8,128)S(1)} %get-tuple-element.23), channel_id=1, source_target_pairs={{0,16},{8,24},{16,0},{24,8},{1,17},{9,25},{17,1},{25,9},{2,18},{10... | collective-permute-start | bytes 196616 | tf_op jit(solution)/shard_map/ppermute | solution.py:22
  49.1 1.6 %collective-permute-done.22.refs_2_ = f32[4,32,128]{2,1,0:T(8,128)S(1)} collective-permute-done((f32[4,32,128]{2,1,0:T(8,128)S(1)}, f32[4,32,128]{2,1,0:T(8,128)S(1)}, u32[]{:S(2)}, u32[]{:S(2)}) %collective-permute-start.22) | collective-permute-done | bytes 65568 | tf_op jit(solution)/shard_map/ppermute | solution.py:22
  50.7 1.2 %collective-permute-start.23 = (f32[4,32,128]{2,1,0:T(8,128)S(1)}, f32[4,32,128]{2,1,0:T(8,128)S(1)}, u32[]{:S(2)}, u32[]{:S(2)}) collective-permute-start(f32[4,32,128]{2,1,0:T(8,128)S(1)} %get-tuple-element.24), channel_id=1, source_target_pairs={{0,24},{8,16},{16,8},{24,0},{1,25},{9,17},{17,9},{25,1},{2,26},{10... | collective-permute-start | bytes 196616 | tf_op jit(solution)/shard_map/ppermute | solution.py:22
  52.0 3.8 %collective-permute-done.23.refs_3_ = f32[4,32,128]{2,1,0:T(8,128)S(1)} collective-permute-done((f32[4,32,128]{2,1,0:T(8,128)S(1)}, f32[4,32,128]{2,1,0:T(8,128)S(1)}, u32[]{:S(2)}, u32[]{:S(2)}) %collective-permute-start.23) | collective-permute-done | bytes 65568 | tf_op jit(solution)/shard_map/ppermute | solution.py:22
  55.8 1.0 %collective-permute-start.20 = (f32[2,4,16,128]{3,2,1,0:T(8,128)S(1)}, f32[2,4,16,128]{3,2,1,0:T(8,128)S(1)}, u32[]{:S(2)}, u32[]{:S(2)}) collective-permute-start(f32[2,4,16,128]{3,2,1,0:T(8,128)S(1)} %get-tuple-element.28), channel_id=1, source_target_pairs={{0,6},{1,7},{2,4},{3,5},{4,2},{5,3},{6,0},{7,1},{8,14},{9,15},{10,... | collective-permute-start | bytes 196616 | tf_op jit(solution)/shard_map/ppermute | solution.py:22
  57.7 4.2 %collective-permute-done.20.refs_11_ = f32[2,4,16,128]{3,2,1,0:T(8,128)S(1)} collective-permute-done((f32[2,4,16,128]{3,2,1,0:T(8,128)S(1)}, f32[2,4,16,128]{3,2,1,0:T(8,128)S(1)}, u32[]{:S(2)}, u32[]{:S(2)}) %collective-permute-start.20) | collective-permute-done | bytes 65568 | tf_op jit(solution)/shard_map/ppermute | solution.py:22
  61.9 5.4 %shard_map.106 = f32[4,16,128]{2,1,0:T(8,128)} custom-call(s32[8]{0:T(128)S(1)} %copy-done.7, s32[8]{0:T(128)S(1)} %convert_reduce_fusion.cells, f32[8,8]{1,0:T(8,128)S(1)} %slice.53.traces, f32[8,64,128]{2,1,0:T(8,128)S(1)} %pad_maximum_fusion.refs_0_, f32[8,64,128]{2,1,0:T(8,128)S(1)} %collective-permute-done.4.refs_1_, ...), custom_call_target="tpu_custom_call" | custom-call | flops 31457280 | bytes 2392064 | tf_op jit(solution)/shard_map/pallas_call | solution.py:32
  (83 shorter events, 10.6 us)
Async XLA Ops:
  7.9 4.5 %collective-permute-start = (f32[520,128]{1,0:T(8,128)S(1)}, f32[520,128]{1,0:T(8,128)}, u32[]{:S(2)}, u32[]{:S(2)}) collective-permute-start(f32[520,128]{1,0:T(8,128)S(1)} %get-tuple-element.15), channel_id=1, source_target_pairs={{0,1},{1,0},{2,3},{3,2},{4,5},{5,4},{6,7},{7,6},{8,9},{9,8},{10,11... | collective-permute-start | bytes 798728 | tf_op jit(solution)/shard_map/ppermute | solution.py:22
  8.4 12.3 %collective-permute-start.7 = (f32[12,64,128]{2,1,0:T(8,128)S(1)}, f32[12,64,128]{2,1,0:T(8,128)S(1)}, u32[]{:S(2)}, u32[]{:S(2)}) collective-permute-start(f32[12,64,128]{2,1,0:T(8,128)S(1)} %get-tuple-element.18), channel_id=1, source_target_pairs={{0,8},{8,0},{16,24},{24,16},{1,9},{9,1},{17,25},{25,17},{2,10},{10... | collective-permute-start | bytes 1179656 | tf_op jit(solution)/shard_map/ppermute | solution.py:22
  10.9 20.6 %collective-permute-start.8 = (f32[12,64,128]{2,1,0:T(8,128)}, f32[12,64,128]{2,1,0:T(8,128)S(1)}, u32[]{:S(2)}, u32[]{:S(2)}) collective-permute-start(f32[12,64,128]{2,1,0:T(8,128)} %get-tuple-element.19), channel_id=1, source_target_pairs={{0,16},{8,24},{16,0},{24,8},{1,17},{9,25},{17,1},{25,9},{2,18},{10... | collective-permute-start | bytes 1179656 | tf_op jit(solution)/shard_map/ppermute | solution.py:22
  14.2 9.1 %collective-permute-start.1 = (f32[264,128]{1,0:T(8,128)S(1)}, f32[264,128]{1,0:T(8,128)S(1)}, u32[]{:S(2)}, u32[]{:S(2)}) collective-permute-start(f32[264,128]{1,0:T(8,128)S(1)} %get-tuple-element.38), channel_id=1, source_target_pairs={{0,2},{1,3},{2,0},{3,1},{4,6},{5,7},{6,4},{7,5},{8,10},{9,11},{10,... | collective-permute-start | bytes 405512 | tf_op jit(solution)/shard_map/ppermute | solution.py:22
  15.9 13.1 %collective-permute-start.2 = (f32[264,128]{1,0:T(8,128)S(1)}, f32[264,128]{1,0:T(8,128)S(1)}, u32[]{:S(2)}, u32[]{:S(2)}) collective-permute-start(f32[264,128]{1,0:T(8,128)S(1)} %get-tuple-element.39), channel_id=1, source_target_pairs={{0,4},{1,5},{2,6},{3,7},{4,0},{5,1},{6,2},{7,3},{8,12},{9,13},{10,... | collective-permute-start | bytes 405512 | tf_op jit(solution)/shard_map/ppermute | solution.py:22
  18.5 10.6 %collective-permute-start.3 = (f32[264,128]{1,0:T(8,128)S(1)}, f32[264,128]{1,0:T(8,128)S(1)}, u32[]{:S(2)}, u32[]{:S(2)}) collective-permute-start(f32[264,128]{1,0:T(8,128)S(1)} %get-tuple-element.40), channel_id=1, source_target_pairs={{0,6},{1,7},{2,4},{3,5},{4,2},{5,3},{6,0},{7,1},{8,14},{9,15},{10,... | collective-permute-start | bytes 405512 | tf_op jit(solution)/shard_map/ppermute | solution.py:22
  20.6 13.3 %collective-permute-start.9 = (f32[12,64,128]{2,1,0:T(8,128)S(1)}, f32[12,64,128]{2,1,0:T(8,128)S(1)}, u32[]{:S(2)}, u32[]{:S(2)}) collective-permute-start(f32[12,64,128]{2,1,0:T(8,128)S(1)} %get-tuple-element.20), channel_id=1, source_target_pairs={{0,24},{8,16},{16,8},{24,0},{1,25},{9,17},{17,9},{25,1},{2,26},{10... | collective-permute-start | bytes 1179656 | tf_op jit(solution)/shard_map/ppermute | solution.py:22
  23.4 7.0 %collective-permute-start.17 = (f32[4,4,16,128]{3,2,0,1:T(8,128)S(1)}, f32[4,4,16,128]{3,2,0,1:T(8,128)}, u32[]{:S(2)}, u32[]{:S(2)}) collective-permute-start(f32[4,4,16,128]{3,2,0,1:T(8,128)S(1)} %bitcast.42), channel_id=1, source_target_pairs={{0,1},{1,0},{2,3},{3,2},{4,5},{5,4},{6,7},{7,6},{8,9},{9,8},{10,11... | collective-permute-start | bytes 393224 | tf_op jit(solution)/shard_map/ppermute | solution.py:22
  29.0 5.0 %collective-permute-start.10 = (f32[4,64,128]{2,1,0:T(8,128)S(1)}, f32[4,64,128]{2,1,0:T(8,128)S(1)}, u32[]{:S(2)}, u32[]{:S(2)}) collective-permute-start(f32[4,64,128]{2,1,0:T(8,128)S(1)} %slice.68), channel_id=1, source_target_pairs={{0,1},{1,0},{2,3},{3,2},{4,5},{5,4},{6,7},{7,6},{8,9},{9,8},{10,11... | collective-permute-start | bytes 393224 | tf_op jit(solution)/shard_map/ppermute | solution.py:22
  29.7 14.9 %collective-permute-start.4 = (f32[8,64,128]{2,1,0:T(8,128)S(1)}, f32[8,64,128]{2,1,0:T(8,128)S(1)}, u32[]{:S(2)}, u32[]{:S(2)}) collective-permute-start(f32[8,64,128]{2,1,0:T(8,128)S(1)} %pad_maximum_fusion.refs_0_), channel_id=1, source_target_pairs={{0,8},{8,0},{16,24},{24,16},{1,9},{9,1},{17,25},{25,17},{2,10},{10... | collective-permute-start | bytes 786440 | tf_op jit(solution)/shard_map/ppermute | solution.py:22
  30.3 16.1 %collective-permute-start.5 = (f32[8,64,128]{2,1,0:T(8,128)S(1)}, f32[8,64,128]{2,1,0:T(8,128)S(1)}, u32[]{:S(2)}, u32[]{:S(2)}) collective-permute-start(f32[8,64,128]{2,1,0:T(8,128)S(1)} %pad_maximum_fusion.refs_0_), channel_id=1, source_target_pairs={{0,16},{8,24},{16,0},{24,8},{1,17},{9,25},{17,1},{25,9},{2,18},{10... | collective-permute-start | bytes 786440 | tf_op jit(solution)/shard_map/ppermute | solution.py:22
  31.4 16.6 %collective-permute-start.6 = (f32[8,64,128]{2,1,0:T(8,128)S(1)}, f32[8,64,128]{2,1,0:T(8,128)S(1)}, u32[]{:S(2)}, u32[]{:S(2)}) collective-permute-start(f32[8,64,128]{2,1,0:T(8,128)S(1)} %pad_maximum_fusion.refs_0_), channel_id=1, source_target_pairs={{0,24},{8,16},{16,8},{24,0},{1,25},{9,17},{17,9},{25,1},{2,26},{10... | collective-permute-start | bytes 786440 | tf_op jit(solution)/shard_map/ppermute | solution.py:22
  34.0 1.8 %collective-permute-start.11 = (f32[4,64,128]{2,1,0:T(8,128)}, f32[4,64,128]{2,1,0:T(8,128)S(1)}, u32[]{:S(2)}, u32[]{:S(2)}) collective-permute-start(f32[4,64,128]{2,1,0:T(8,128)} %slice.69), channel_id=1, source_target_pairs={{0,1},{1,0},{2,3},{3,2},{4,5},{5,4},{6,7},{7,6},{8,9},{9,8},{10,11... | collective-permute-start | bytes 393224 | tf_op jit(solution)/shard_map/ppermute | solution.py:22
  34.0 4.0 %collective-permute-start.12 = (f32[4,64,128]{2,1,0:T(8,128)S(1)}, f32[4,64,128]{2,1,0:T(8,128)S(1)}, u32[]{:S(2)}, u32[]{:S(2)}) collective-permute-start(f32[4,64,128]{2,1,0:T(8,128)S(1)} %slice.70), channel_id=1, source_target_pairs={{0,1},{1,0},{2,3},{3,2},{4,5},{5,4},{6,7},{7,6},{8,9},{9,8},{10,11... | collective-permute-start | bytes 393224 | tf_op jit(solution)/shard_map/ppermute | solution.py:22
  35.8 12.3 %collective-permute-start.18 = (f32[2,4,16,128]{3,2,1,0:T(8,128)S(1)}, f32[2,4,16,128]{3,2,1,0:T(8,128)S(1)}, u32[]{:S(2)}, u32[]{:S(2)}) collective-permute-start(f32[2,4,16,128]{3,2,1,0:T(8,128)S(1)} %get-tuple-element.30), channel_id=1, source_target_pairs={{0,2},{1,3},{2,0},{3,1},{4,6},{5,7},{6,4},{7,5},{8,10},{9,11},{10,... | collective-permute-start | bytes 196616 | tf_op jit(solution)/shard_map/ppermute | solution.py:22
  38.0 10.6 %collective-permute-start.19 = (f32[2,4,16,128]{3,2,1,0:T(8,128)S(1)}, f32[2,4,16,128]{3,2,1,0:T(8,128)S(1)}, u32[]{:S(2)}, u32[]{:S(2)}) collective-permute-start(f32[2,4,16,128]{3,2,1,0:T(8,128)S(1)} %get-tuple-element.31), channel_id=1, source_target_pairs={{0,4},{1,5},{2,6},{3,7},{4,0},{5,1},{6,2},{7,3},{8,12},{9,13},{10,... | collective-permute-start | bytes 196616 | tf_op jit(solution)/shard_map/ppermute | solution.py:22
  44.6 4.3 %collective-permute-start.21 = (f32[4,32,128]{2,1,0:T(8,128)S(1)}, f32[4,32,128]{2,1,0:T(8,128)S(1)}, u32[]{:S(2)}, u32[]{:S(2)}) collective-permute-start(f32[4,32,128]{2,1,0:T(8,128)S(1)} %get-tuple-element.22), channel_id=1, source_target_pairs={{0,8},{8,0},{16,24},{24,16},{1,9},{9,1},{17,25},{25,17},{2,10},{10... | collective-permute-start | bytes 196616 | tf_op jit(solution)/shard_map/ppermute | solution.py:22
  46.4 4.3 %collective-permute-start.22 = (f32[4,32,128]{2,1,0:T(8,128)S(1)}, f32[4,32,128]{2,1,0:T(8,128)S(1)}, u32[]{:S(2)}, u32[]{:S(2)}) collective-permute-start(f32[4,32,128]{2,1,0:T(8,128)S(1)} %get-tuple-element.23), channel_id=1, source_target_pairs={{0,16},{8,24},{16,0},{24,8},{1,17},{9,25},{17,1},{25,9},{2,18},{10... | collective-permute-start | bytes 196616 | tf_op jit(solution)/shard_map/ppermute | solution.py:22
  48.1 13.9 %collective-permute-start.13 = (f32[8,64,128]{2,1,0:T(8,128)S(1)}, f32[8,64,128]{2,1,0:T(8,128)S(1)}, u32[]{:S(2)}, u32[]{:S(2)}) collective-permute-start(f32[8,64,128]{2,1,0:T(8,128)S(1)} %pad_maximum_fusion.refs_0_), channel_id=1, source_target_pairs={{0,1},{1,0},{2,3},{3,2},{4,5},{5,4},{6,7},{7,6},{8,9},{9,8},{10,11... | collective-permute-start | bytes 786440 | tf_op jit(solution)/shard_map/ppermute | solution.py:22
  48.1 13.9 %collective-permute-start.14 = (f32[8,64,128]{2,1,0:T(8,128)S(1)}, f32[8,64,128]{2,1,0:T(8,128)S(1)}, u32[]{:S(2)}, u32[]{:S(2)}) collective-permute-start(f32[8,64,128]{2,1,0:T(8,128)S(1)} %collective-permute-done.4.refs_1_), channel_id=1, source_target_pairs={{0,1},{1,0},{2,3},{3,2},{4,5},{5,4},{6,7},{7,6},{8,9},{9,8},{10,11... | collective-permute-start | bytes 786440 | tf_op jit(solution)/shard_map/ppermute | solution.py:22
  48.6 13.3 %collective-permute-start.15 = (f32[8,64,128]{2,1,0:T(8,128)S(1)}, f32[8,64,128]{2,1,0:T(8,128)S(1)}, u32[]{:S(2)}, u32[]{:S(2)}) collective-permute-start(f32[8,64,128]{2,1,0:T(8,128)S(1)} %collective-permute-done.5.refs_2_), channel_id=1, source_target_pairs={{0,1},{1,0},{2,3},{3,2},{4,5},{5,4},{6,7},{7,6},{8,9},{9,8},{10,11... | collective-permute-start | bytes 786440 | tf_op jit(solution)/shard_map/ppermute | solution.py:22
  49.0 13.0 %collective-permute-start.16 = (f32[8,64,128]{2,1,0:T(8,128)S(1)}, f32[8,64,128]{2,1,0:T(8,128)S(1)}, u32[]{:S(2)}, u32[]{:S(2)}) collective-permute-start(f32[8,64,128]{2,1,0:T(8,128)S(1)} %collective-permute-done.6.refs_3_), channel_id=1, source_target_pairs={{0,1},{1,0},{2,3},{3,2},{4,5},{5,4},{6,7},{7,6},{8,9},{9,8},{10,11... | collective-permute-start | bytes 786440 | tf_op jit(solution)/shard_map/ppermute | solution.py:22
  50.7 5.2 %collective-permute-start.23 = (f32[4,32,128]{2,1,0:T(8,128)S(1)}, f32[4,32,128]{2,1,0:T(8,128)S(1)}, u32[]{:S(2)}, u32[]{:S(2)}) collective-permute-start(f32[4,32,128]{2,1,0:T(8,128)S(1)} %get-tuple-element.24), channel_id=1, source_target_pairs={{0,24},{8,16},{16,8},{24,0},{1,25},{9,17},{17,9},{25,1},{2,26},{10... | collective-permute-start | bytes 196616 | tf_op jit(solution)/shard_map/ppermute | solution.py:22
  55.8 6.1 %collective-permute-start.20 = (f32[2,4,16,128]{3,2,1,0:T(8,128)S(1)}, f32[2,4,16,128]{3,2,1,0:T(8,128)S(1)}, u32[]{:S(2)}, u32[]{:S(2)}) collective-permute-start(f32[2,4,16,128]{3,2,1,0:T(8,128)S(1)} %get-tuple-element.28), channel_id=1, source_target_pairs={{0,6},{1,7},{2,4},{3,5},{4,2},{5,3},{6,0},{7,1},{8,14},{9,15},{10,... | collective-permute-start | bytes 196616 | tf_op jit(solution)/shard_map/ppermute | solution.py:22
  (18 other events, 89.0 us)

commit v2 on v1

--- a/solution.py
+++ b/solution.py
@@ -15,6 +15,7 @@
 
 VMEM = pl.BlockSpec(memory_space=pltpu.VMEM)
 SMEM = pl.BlockSpec(memory_space=pltpu.SMEM)
+HBM = pl.BlockSpec(memory_space=pltpu.HBM)
 
 
 def swap(block, axis, mask):
@@ -26,18 +27,33 @@
     return functools.reduce(lambda a, b: a * b, shape)
 
 
-def call(body, outs, inputs, scalars, scratch, flops=0):
-    size = 4 * (sum(x.size for x in inputs) + sum(count(o) for o in outs))
-    held = sum(count(s.shape) * 4 for s in scratch)
-    return pl.pallas_call(
+def call(body, outs, inputs, scalars, scratch, flops=0, far=()):
+    size = 4 * (sum(x.size for x in (*inputs, *far)) + sum(count(o) for o in outs))
+    held = sum(count(s.shape) * 4 for s in scratch if hasattr(s, "shape"))
+    launch = pl.pallas_call(
         body,
         out_shape=[jax.ShapeDtypeStruct(o, jnp.float32) for o in outs],
-        in_specs=[SMEM] * len(scalars) + [VMEM] * len(inputs),
+        in_specs=[SMEM] * len(scalars) + [HBM] * len(far) + [VMEM] * len(inputs),
         out_specs=[VMEM] * len(outs),
         scratch_shapes=scratch,
         cost_estimate=pl.CostEstimate(flops=flops, bytes_accessed=size, transcendentals=0),
         compiler_params=pltpu.CompilerParams(vmem_limit_bytes=size + held + SPARE),
-    )(*scalars, *inputs)
+    )
+    far = [pltpu.with_memory_space_constraint(x, pltpu.HBM) for x in far]
+    return launch(*scalars, *far, *inputs)
+
+
+def plan_rows(size_y, slabs, halo):
+    inner = size_y - 2 * halo
+    if inner > 0 and inner % (8 * slabs) == 0:
+        stride = inner // slabs
+        return stride, 0, stride + 2 * halo, stride + halo
+    share = size_y // slabs
+    return share, -halo, share + 2 * halo, share
+
+
+def masks(chips):
+    return [2**bit for bit in reversed(range(chips.bit_length() - 1))]
 
 
 def position():
@@ -171,29 +187,48 @@
     return low // 8 * 8, min(rows, -(-high // 8) * 8)
 
 
-def pack_body(dims, cells, traces, weights, now, old, courant, logb, *refs):
-    slabs, planes, size_y, size_z, share, halo, steps = dims
-    own, sent, whole, *outs, wide = refs
-    window = share + 2 * halo
+def pack_body(dims, cells, weights, courant, logb, now, old, store, traces, *refs):
+    slabs, planes, size_y, size_z, rows_of, tile, halo, steps = dims
+    own, sent, kept, given, model, whole, *outs, wide, shot, trace, sems = refs
+    stride, begin, window, _ = rows_of
     half = planes // 2
-    slab, core, _ = position()
+    slab, core, chip = position()
     weight = weights[0]
-    for i, ref in enumerate((now, old)):
+    inner = pl.ds(halo, size_y)
+    copies = [
+        pltpu.make_async_copy(ref, wide.at[i, :, inner, :], sems.at[i]) for i, ref in enumerate((courant, logb, now, old))
+    ]
+    copies += [pltpu.make_async_copy(store, shot, sems.at[4]), pltpu.make_async_copy(traces, trace, sems.at[5])]
+    for i in (2, 3, 5, 4, 0, 1):
+        copies[i].start()
+    wide[:, :, 0:halo, :] = jnp.zeros((4, planes, halo, size_z), jnp.float32)
+    wide[:, :, halo + size_y :, :] = jnp.zeros((4, planes, halo, size_z), jnp.float32)
+    for i in (2, 3):
+        copies[i].wait()
         for j in range(half):
-            own[i, j] = weight * ref[half * core + j]
-            sent[pl.ds((i * half + j) * size_y, size_y), :] = weight * ref[half * (1 - core) + j]
-    lane = lax.broadcasted_iota(jnp.int32, (8, size_z), 1)
-    sub = lax.broadcasted_iota(jnp.int32, (8, size_z), 0)
+            own[i - 2, j] = weight * wide[i, half * core + j, halo : halo + size_y, :]
+            row = ((i - 2) * half + j) * size_y
+            sent[row : row + size_y, :] = weight * wide[i, half * (1 - core) + j, halo : halo + size_y, :]
+    copies[5].wait()
+    ranks = size_y // tile
+    lane = lax.broadcasted_iota(jnp.int32, (ranks, size_z), 1)
+    sub = lax.broadcasted_iota(jnp.int32, (ranks, size_z), 0)
     row = jnp.where(lane == 0, cells[0].astype(jnp.float32), 0.0)
     for step in range(steps):
-        row = jnp.where(lane == 1 + step, weight * traces[0, step], row)
-    sent[pl.ds(2 * half * size_y, 8), :] = jnp.where(sub == core, row, 0.0)
-    wide[:, :, 0:halo, :] = jnp.zeros((4, planes, halo, size_z), jnp.float32)
-    wide[:, :, halo + size_y :, :] = jnp.zeros((4, planes, halo, size_z), jnp.float32)
-    for i, ref in enumerate((courant, logb, now, old)):
-        wide[i, :, halo : halo + size_y, :] = ref[...]
+        row = jnp.where(lane == 1 + step, weight * trace[0, step], row)
+    sent[2 * half * size_y :, :] = jnp.where(sub == 2 * chip + core, row, 0.0)
+    copies[4].wait()
+    for j in range(size_y // (2 * tile)):
+        first, second = [shot[:, (2 * j + i) * tile : (2 * j + i + 1) * tile, :] for i in range(2)]
+        kept[:, j] = jnp.where(core == 0, first, second)
+        given[:, j] = jnp.where(core == 0, second, first)
+    for i in (0, 1):
+        copies[i].wait()
+    for i in range(2):
+        rows = pl.ds(pl.multiple_of(chip * 2 * tile, 8), 2 * tile + 2 * halo)
+        model[i * half : (i + 1) * half] = wide[i, pl.ds(half * core, half), rows, :]
     for d in range(slabs):
-        rows = pl.ds(pl.multiple_of((slab ^ d) * share, 8), window)
+        rows = pl.ds(pl.multiple_of((slab ^ d) * stride + begin + halo, 8), window)
         if d == 0:
             for i in range(4):
                 whole[i * planes : (i + 1) * planes] = wide[i, :, rows, :]
@@ -204,14 +239,74 @@
             out[2 * half + i * planes : 2 * half + (i + 1) * planes] = wide[2 + i, :, rows, :]
 
 
+def halves(chip, mask):
+    upper = (chip // mask) % 2
+    return upper, 1 - upper
+
+
+def pair_body(dims, own, sent, got, keep, send, wide):
+    chips, half, size_y, tile, halo = dims
+    rows = chips * tile + halo
+    cut = 2 * half * size_y
+    sides = halves(position()[2], chips // 2)
+    for i in range(2 * half):
+        wide[i] = own[i // half, i % half] + got[i * size_y : (i + 1) * size_y, :]
+    for out, side in zip((keep, send), sides):
+        taken = pl.ds(pl.multiple_of(side * (size_y - rows), 8), rows)
+        for i in range(2 * half):
+            out[i * rows : (i + 1) * rows, :] = wide[i, taken, :]
+        out[2 * half * rows :, :] = sent[cut:, :] + got[cut:, :]
+
+
+def halve_body(dims, held, got, keep, send, wide):
+    chips, half, tile, halo, mask = dims
+    whole = 4 * mask * tile + 2 * halo
+    edge = 2 * mask == chips // 2
+    before = whole - halo if edge else whole
+    rows = 2 * mask * tile + 2 * halo
+    chip = position()[2]
+    offset = 0
+    if edge:
+        wide[...] = jnp.zeros(wide.shape, jnp.float32)
+        offset = pl.multiple_of(halo * halves(chip, 2 * mask)[1], 8)
+    for i in range(2 * half):
+        part = slice(i * before, (i + 1) * before)
+        wide[i, pl.ds(offset, before), :] = held[part, :] + got[part, :]
+    for out, side in zip((keep, send), halves(chip, mask)):
+        taken = pl.ds(pl.multiple_of(side * 2 * mask * tile, 8), rows)
+        for i in range(2 * half):
+            out[i * rows : (i + 1) * rows, :] = wide[i, taken, :]
+        out[2 * half * rows :, :] = held[2 * half * before :, :] + got[2 * half * before :, :]
+
+
+def shot_body(mask, held, got, keep, send):
+    for out, side in zip((keep, send), halves(position()[2], mask)):
+        taken = pl.ds(side * mask, mask)
+        if len(held.shape) == 4:
+            out[0], out[1] = held[:, taken], got[:, taken]
+        else:
+            out[: held.shape[0]], out[held.shape[0] :] = held[:, :, taken], got[:, :, taken]
+
+
+def total_body(dims, model, held, got, out, infos):
+    half, rows = dims
+    for i in range(2 * half):
+        taken = slice(i * rows, (i + 1) * rows)
+        out[i] = held[taken, :] + got[taken, :]
+    out[2 * half :] = model[...]
+    infos[...] = held[2 * half * rows :, :] + got[2 * half * rows :, :]
+
+
 def field_body(dims, cells, traces, whole, *refs):
-    slabs, planes, size_y, size_z, share, halo, steps = dims
-    window = share + 2 * halo
+    slabs, planes, size_y, size_z, rows_of, halo, steps = dims
+    stride, begin, window, given = rows_of
     half = planes // 2
     total = planes * slabs
     blocks, others, outs = refs[: slabs - 1], refs[slabs - 1 : 2 * slabs - 2], refs[2 * slabs - 2 : 3 * slabs - 2]
-    now, old, c_ref, b_ref, coef, *bands = refs[3 * slabs - 2 :]
+    trace, sem, now, old, c_ref, b_ref, coef, *bands = refs[3 * slabs - 2 :]
     slab, core, _ = position()
+    copy = pltpu.make_async_copy(traces, trace, sem.at[0])
+    copy.start()
     clear_edges((now, old, c_ref, b_ref), window)
     fill_bands(*bands)
     inner = slice(0, window)
@@ -228,34 +323,39 @@
             ref[pl.ds(base + half * core, half), inner, :] = blocks[d - 1][i * half : (i + 1) * half]
             ref[pl.ds(base + half * (1 - core), half), inner, :] = others[d - 1][i * half : (i + 1) * half]
     prepare(c_ref, b_ref, coef, bands, total)
-    spot = place(cells[0], slab * share - halo, size_y, size_z)
+    spot = place(cells[0], slab * stride + begin, size_y, size_z)
+    copy.wait()
     for step in range(steps):
-        low, high = span(step, window)
+        low, high = span(step, window) if begin else (0, window)
         advance(now, old, coef, bands, low, high, total)
 
         @pl.when((spot[1] >= 0) & (spot[1] < window))
         def _(target=old, step=step):
-            inject(target, spot, traces[0, step])
+            inject(target, spot, trace[0, step])
 
         now, old = old, now
+    top = halo if begin else pl.multiple_of(jnp.where(slab == 0, 0, halo), 8)
     for d in range(slabs):
-        outs[d][...] = now[pl.ds((slab ^ d) * planes + 2, planes), halo : halo + share, :]
+        outs[d][...] = now[pl.ds((slab ^ d) * planes + 2, planes), pl.ds(top, given), :]
 
 
 def sub_rows(tile, halo):
     return 2 * halo + (tile if tile % 8 == 0 else 2 * tile)
 
 
-def sum_body(dims, order, cells, traces, *refs):
+def sum_body(dims, order, infos, *refs):
     slabs, planes, size_y, size_z, tile, halo, steps, groups = dims
     window = sub_rows(tile, halo)
     half = planes // 2
     total = planes * slabs
-    mine, others, shots = refs[:slabs], refs[slabs : 2 * slabs], refs[2 * slabs : 2 * slabs + groups]
-    out, spots, snaps, now, old, c_ref, b_ref, coef, *bands = refs[2 * slabs + groups :]
+    mine, others, shots = refs[:slabs], refs[slabs : 2 * slabs], refs[2 * slabs : 2 * slabs + 2]
+    out, spots, info, slots, sem, snaps, now, old, c_ref, b_ref, coef, *bands = refs[2 * slabs + 2 :]
     slab, core, chip = position()
-    for d in range(groups):
-        snaps[2 * d : 2 * d + 2] = shots[d][...]
+    copies = [pltpu.make_async_copy(infos, info, sem.at[0]), pltpu.make_async_copy(order, slots, sem.at[1])]
+    for copy in copies:
+        copy.start()
+    for d in range(2):
+        snaps[d * groups : (d + 1) * groups] = shots[d][:, :, 0]
     clear_edges((now, old, c_ref, b_ref), window)
     fill_bands(*bands)
     inner = slice(0, window)
@@ -269,8 +369,11 @@
     prepare(c_ref, b_ref, coef, bands, total)
     first = chip * 2 * tile - halo + offset
 
+    for copy in copies:
+        copy.wait()
+
     def note(r, found):
-        spot = place(cells[r], first, size_y, size_z)
+        spot = place(info[r, 0].astype(jnp.int32), first, size_y, size_z)
         for i, value in enumerate(spot + (r,)):
             spots[i, found] = value
         return found + ((spot[1] >= 0) & (spot[1] < window)).astype(jnp.int32)
@@ -285,14 +388,17 @@
             advance(now, old, coef, bands, low, high, total)
 
         def add(i, carry, target=old, step=step):
-            inject(target, (spots[0, i], spots[1, i], spots[2, i]), traces[spots[3, i], step])
+            inject(target, (spots[0, i], spots[1, i], spots[2, i]), info[spots[3, i], 1 + step])
             return carry
 
         lax.fori_loop(0, inside, add, 0)
         now, old = old, now
         if step % 2 == 1:
-            slot = order[step // 2]
-            piece = ((slot // 2) ^ chip) * 2 + ((slot % 2) ^ core)
+            slot = slots[step // 2]
+            away = (slot // 2) ^ chip
+            piece = (slot % 2) ^ core
+            for bit in range(groups.bit_length() - 1):
+                piece = piece + ((away // 2**bit) % 2) * (groups // 2**bit)
             own = pl.ds(slab * planes + 2, planes)
             top = halo
             field = now[own, top : top + tile, :]
@@ -303,11 +409,21 @@
 
 
 def unpack_body(dims, *refs):
-    slabs, share = dims
+    slabs, rows_of, halo = dims
+    stride, begin, _, given = rows_of
     out = refs[slabs]
     slab, _, _ = position()
     for d in range(slabs):
-        out[:, pl.ds(pl.multiple_of((slab ^ d) * share, 8), share), :] = refs[d][...]
+        peer = slab ^ d
+        if begin:
+            out[:, pl.ds(pl.multiple_of(peer * stride, 8), given), :] = refs[d][...]
+            continue
+        top = pl.multiple_of(peer * stride + jnp.where(peer == 0, 0, halo), 8)
+        out[:, pl.ds(top, stride), :] = refs[d][:, :stride, :]
+
+        @pl.when((peer == 0) | (peer == slabs - 1))
+        def _(top=top, piece=refs[d]):
+            out[:, pl.ds(pl.multiple_of(top + stride, 8), halo), :] = piece[:, stride:, :]
 
 
 def local(
@@ -326,56 +442,68 @@
     slabs, ranks = lax.axis_size("slab"), lax.axis_size("rcv")
     chips = ranks // 2
     halo = 2 * steps
-    share = size_y // slabs
+    rows_of = plan_rows(size_y, slabs, halo)
     tile = size_y // ranks
     half = planes // 2
-    window = share + 2 * halo
+    _, _, window, returned = rows_of
     wide = 2 * tile + 2 * halo
     total = planes * slabs
-    rank = lax.axis_index("rcv")
-    core, chip = rank % 2, rank // 2
-    now, old, store = adjoint_now[0], adjoint_before[0], snapshot_store[0]
-
-    cut = 2 * half * size_y
-    own, sent, whole, *blocks = call(
-        functools.partial(pack_body, (slabs, planes, size_y, size_z, share, halo, steps)),
-        [(2, half, size_y, size_z), (cut + 8, size_z), (4 * planes, window, size_z)]
+
+    own, sent, kept, given, model, whole, *blocks = call(
+        functools.partial(pack_body, (slabs, planes, size_y, size_z, rows_of, tile, halo, steps)),
+        [(2, half, size_y, size_z), (2 * half * size_y + ranks, size_z)]
+        + [(planes, chips, tile, size_z)] * 2
+        + [(2 * half, wide, size_z), (4 * planes, window, size_z)]
         + [(2 * half + 2 * planes, window, size_z)] * (slabs - 1),
-        [now, old, courant_field, log_buoyancy],
-        [receiver_cells, receiver_traces, residual_weights],
-        [pltpu.VMEM((4, planes, size_y + 2 * halo, size_z), jnp.float32)],
+        [],
+        [receiver_cells, residual_weights],
+        [
+            pltpu.VMEM((4, planes, size_y + 2 * halo, size_z), jnp.float32),
+            pltpu.VMEM((planes, size_y, size_z), jnp.float32),
+            pltpu.SMEM((1, steps), jnp.float32),
+            pltpu.SemaphoreType.DMA((6,)),
+        ],
+        far=[courant_field, log_buoyancy, adjoint_now[0], adjoint_before[0], snapshot_store[0], receiver_traces],
     )
     got = swap(sent, "rcv", 1)
     blocks = [swap(block, "slab", d + 1) for d, block in enumerate(blocks)]
     others = [swap(block[: 2 * half], "rcv", 1) for block in blocks]
 
-    flat = lambda a: a.reshape(-1, size_z)
-    pair = own + got[:cut].reshape(2, half, size_y, size_z)
-    pair = jnp.pad(pair, ((0, 0), (0, 0), (halo, halo), (0, 0)))
-    info = sent[cut:] + got[cut:]
-    received = []
-    for d in range(chips):
-        rows = lax.dynamic_slice_in_dim(pair, (chip ^ d) * 2 * tile, wide, 2)
-        block = jnp.concatenate([flat(rows), info])
-        received.append(swap(block, "rcv", 2 * d) if d else block)
-    cut = 2 * half * wide
-    summed = functools.reduce(jnp.add, [b[:cut] for b in received]).reshape(2 * half, wide, size_z)
-    infos = jnp.concatenate([b[cut : cut + 2] for b in received])
-    all_cells = infos[:, 0].astype(jnp.int32)
-    all_traces = infos[:, 1 : 1 + steps]
-
-    pick = functools.partial(lax.dynamic_index_in_dim, keepdims=False)
-    tiles = store.reshape(planes, chips, 2, tile, size_z)
-    tiles = jnp.stack([pick(tiles, core, 2), swap(pick(tiles, 1 - core, 2), "rcv", 1)])
-    snaps = [pick(tiles, chip ^ d, 2) for d in range(chips)]
-    snaps = [snaps[0]] + [swap(snaps[d], "rcv", 2 * d) for d in range(1, chips)]
-
-    model = jnp.stack([courant_field, log_buoyancy])
-    model = lax.dynamic_slice_in_dim(model, half * core, half, 1)
-    model = jnp.pad(model, ((0, 0), (0, 0), (halo, halo), (0, 0)))
-    model = lax.dynamic_slice_in_dim(model, chip * 2 * tile, wide, 2)
-    block = jnp.concatenate([summed, model.reshape(2 * half, wide, size_z)])
+    depth = 2 * half
+    rows = chips * tile + halo
+    held, block = call(
+        functools.partial(pair_body, (chips, half, size_y, tile, halo)),
+        [(depth * rows + ranks, size_z)] * 2,
+        [own, sent, got],
+        [],
+        [pltpu.VMEM((depth, size_y, size_z), jnp.float32)],
+    )
+    got = swap(block, "rcv", chips)
+    for mask in masks(chips)[1:]:
+        rows = 2 * mask * tile + 2 * halo
+        held, block = call(
+            functools.partial(halve_body, (chips, half, tile, halo, mask)),
+            [(depth * rows + ranks, size_z)] * 2,
+            [held, got],
+            [],
+            [pltpu.VMEM((depth, 4 * mask * tile + 2 * halo, size_z), jnp.float32)],
+        )
+        got = swap(block, "rcv", 2 * mask)
+    block, infos = call(
+        functools.partial(total_body, (half, wide)),
+        [(4 * half, wide, size_z), (ranks, size_z)],
+        [model, held, got],
+        [],
+        [],
+    )
     mine = [block] + [swap(block, "slab", d) for d in range(1, slabs)]
+
+    snaps = [kept, swap(given, "rcv", 1)]
+    for mask in masks(chips):
+        held, block = call(
+            functools.partial(shot_body, mask), [(chips // mask, planes, mask, tile, size_z)] * 2, snaps, [], []
+        )
+        snaps = [held, swap(block, "rcv", 2 * mask)]
 
     def scratch(rows):
         rows = -(-rows // 16) * 16
@@ -386,11 +514,12 @@
         )
 
     finals = call(
-        functools.partial(field_body, (slabs, planes, size_y, size_z, share, halo, steps)),
-        [(planes, share, size_z)] * slabs,
+        functools.partial(field_body, (slabs, planes, size_y, size_z, rows_of, halo, steps)),
+        [(planes, returned, size_z)] * slabs,
         [whole] + blocks + others,
-        [receiver_cells, receiver_traces],
-        scratch(window),
+        [receiver_cells],
+        [pltpu.SMEM((1, steps), jnp.float32), pltpu.SemaphoreType.DMA((1,))] + scratch(window),
+        far=[receiver_traces],
         flops=40 * steps * total * window * size_z,
     )
     mine[1:] = lax.optimization_barrier(tuple(mine[1:]) + tuple(finals))[: slabs - 1]
@@ -399,13 +528,20 @@
     (sensitivity,) = call(
         functools.partial(sum_body, (slabs, planes, size_y, size_z, tile, halo, steps, chips)),
         [(planes, tile, size_z)],
-        mine + theirs + snaps,
-        [owner_order, all_cells, all_traces],
-        [pltpu.SMEM((4, 2 * chips + 1), jnp.int32), pltpu.VMEM((2 * chips, planes, tile, size_z), jnp.float32)]
+        [infos] + mine + theirs + snaps,
+        [],
+        [
+            pltpu.SMEM((4, 2 * chips + 1), jnp.int32),
+            pltpu.SMEM((2 * chips, size_z), jnp.float32),
+            pltpu.SMEM(owner_order.shape, jnp.int32),
+            pltpu.SemaphoreType.DMA((2,)),
+            pltpu.VMEM((2 * chips, planes, tile, size_z), jnp.float32),
+        ]
         + scratch(sub_rows(tile, halo)),
+        far=[owner_order],
         flops=40 * steps * total * sub_rows(tile, halo) * size_z,
     )
-    (after,) = call(functools.partial(unpack_body, (slabs, share)), [(planes, size_y, size_z)], back, [], [])
+    (after,) = call(functools.partial(unpack_body, (slabs, rows_of, halo)), [(planes, size_y, size_z)], back, [], [])
     return (sensitivity, after[None])
 
 

time: 67.7 us -> 56.6 us (0.84)
  local copies, waits for them, and re-layouts: 7.89 us -> 0.03 us
  starting transfers between devices: 25.9 us -> 22.4 us
  waiting for transfers between devices: 16.8 us -> 20.1 us
  other arithmetic: 1.82 us -> 0 us
  Pallas kernels: 12.8 us -> 11.8 us
    unnamed x28 -> x0, local copies, waits for them, and re-layouts: 5.4 us -> none
    ppermute x24 -> x22, starting transfers between devices: 25.9 us -> 22.4 us  [swap(): return lax.ppermute(block, axis, [(i, i ^ mask) for i in range(peers)])]
    ppermute x24 -> x22, waiting for transfers between devices: 16.8 us -> 20.1 us  [swap(): return lax.ppermute(block, axis, [(i, i ^ mask) for i in range(peers)])]
    slice x10 -> x0, local copies, waits for them, and re-layouts: 1.06 us -> none  [the longest x1 0.97 us: local(): pair = own + got[:cut].reshape(2, half, size_y, size_z)]
    pallas_call x4 -> x9, Pallas kernels: 12.8 us -> 11.8 us  [call(): return launch(*scalars, *far, *inputs)]
    squeeze x1 -> x0, other arithmetic: 0.85 us -> none  [local(): snaps = [pick(tiles, chip ^ d, 2) for d in range(chips)]]
    add x3 -> x0, other arithmetic: 0.78 us -> none  [the longest x1 0.69 us: local(): info = sent[cut:] + got[cut:]]
    dynamic_slice x5 -> x0, local copies, waits for them, and re-layouts: 0.76 us -> none  [the longest x2 0.67 us: local(): pick(tiles, 1 - core, 2)]
  transfers between devices with their start and end apart: 24 -> 22, of which waited for: 6 -> 9; matrix products, arithmetic and copies ran while one was open for 6% -> 0% of each run, Pallas kernels for 9% -> 10%
where the time goes in v2:
time: 56.6 us; the launch traced here: 56.4 us
  starting transfers between devices  22.4 us (40%)
  waiting for transfers between devices  20.1 us (36%)
  Pallas kernels  11.8 us (21%)
  between operations  2.04 us (4%)
    ppermute x22, starting transfers between devices, swap(): return lax.ppermute(block, axis, [(i, i ^ mask) for i in range(peers)])  22.4 us
    ppermute x22, waiting for transfers between devices, swap(): return lax.ppermute(block, axis, [(i, i ^ mask) for i in range(peers)])  20.1 us
    pallas_call x9, Pallas kernels, call(): return launch(*scalars, *far, *inputs)  11.8 us
  transfers between devices with their start and end apart: 22, of which 9 were waited for; matrix products, arithmetic and copies ran while one was open for 0% of the time, Pallas kernels for 10%

profile of v2, /device:TPU:0, one launch (start us, length us, event | category | flops | bytes accessed | tf_op | source)
XLA Modules:
  0.0 56.4 jit_solution(10809951888350076227)
XLA Ops:
  1.9 1.4 %shard_map.104 = (f32[2,2,128,128]{3,2,1,0:T(8,128)S(1)}, f32[520,128]{1,0:T(8,128)S(1)}, f32[4,4,16,128]{3,2,1,0:T(8,128)S(1)}, f32[4,4,16,128]{3,2,1,0:T(8,128...) custom-call(s32[1]{0:T(128)S(6)} %copy.11.cells, ...), custom_call_target="tpu_custom_call" | custom-call | bytes 3723296 | tf_op jit(solution)/shard_map/pallas_call | solution.py:43
  3.4 0.6 collective-permute-start
  3.9 2.6 %collective-permute-start.7 = (f32[12,56,128]{2,1,0:T(8,128)S(1)}, f32[12,56,128]{2,1,0:T(8,128)S(1)}, u32[]{:S(2)}, u32[]{:S(2)}) collective-permute-start(f32[12,56,128]{2,1,0:T(8,128)S(1)} %get-tuple-element.39), channel_id=1, source_target_pairs={{0,16},{8,24},{16,0},{24,8},{1,17},{9,25},{17,1},{25,9},{2,18},{10... | collective-permute-start | bytes 1032200 | tf_op jit(solution)/shard_map/ppermute | solution.py:23
  6.5 1.4 %collective-permute-start.8 = (f32[12,56,128]{2,1,0:T(8,128)S(1)}, f32[12,56,128]{2,1,0:T(8,128)S(1)}, u32[]{:S(2)}, u32[]{:S(2)}) collective-permute-start(f32[12,56,128]{2,1,0:T(8,128)S(1)} %get-tuple-element.40), channel_id=1, source_target_pairs={{0,24},{8,16},{16,8},{24,0},{1,25},{9,17},{17,9},{25,1},{2,26},{10... | collective-permute-start | bytes 1032200 | tf_op jit(solution)/shard_map/ppermute | solution.py:23
  8.0 2.7 %collective-permute-start.1 = (f32[328,128]{1,0:T(8,128)S(1)}, f32[328,128]{1,0:T(8,128)S(1)}, u32[]{:S(2)}, u32[]{:S(2)}) collective-permute-start(f32[328,128]{1,0:T(8,128)S(1)} %get-tuple-element.32), channel_id=1, source_target_pairs={{0,4},{1,5},{2,6},{3,7},{4,0},{5,1},{6,2},{7,3},{8,12},{9,13},{10,... | collective-permute-start | bytes 503816 | tf_op jit(solution)/shard_map/ppermute | solution.py:23
  11.2 7.4 %collective-permute-done.1.got = f32[328,128]{1,0:T(8,128)S(1)} collective-permute-done((f32[328,128]{1,0:T(8,128)S(1)}, f32[328,128]{1,0:T(8,128)S(1)}, u32[]{:S(2)}, u32[]{:S(2)}) %collective-permute-start.1) | collective-permute-done | bytes 167968 | tf_op jit(solution)/shard_map/ppermute | solution.py:23
  18.7 0.7 %collective-permute-start.2 = (f32[264,128]{1,0:T(8,128)S(1)}, f32[264,128]{1,0:T(8,128)S(1)}, u32[]{:S(2)}, u32[]{:S(2)}) collective-permute-start(f32[264,128]{1,0:T(8,128)S(1)} %get-tuple-element.34), channel_id=1, source_target_pairs={{0,2},{1,3},{2,0},{3,1},{4,6},{5,7},{6,4},{7,5},{8,10},{9,11},{10,... | collective-permute-start | bytes 405512 | tf_op jit(solution)/shard_map/ppermute | solution.py:23
  19.4 3.1 %collective-permute-done.7.refs_1_ = f32[12,56,128]{2,1,0:T(8,128)S(1)} collective-permute-done((f32[12,56,128]{2,1,0:T(8,128)S(1)}, f32[12,56,128]{2,1,0:T(8,128)S(1)}, u32[]{:S(2)}, u32[]{:S(2)}) %collective-permute-start.7) | collective-permute-done | bytes 344096 | tf_op jit(solution)/shard_map/ppermute | solution.py:23
  22.6 1.1 %collective-permute-done.2.got = f32[264,128]{1,0:T(8,128)S(1)} collective-permute-done((f32[264,128]{1,0:T(8,128)S(1)}, f32[264,128]{1,0:T(8,128)S(1)}, u32[]{:S(2)}, u32[]{:S(2)}) %collective-permute-start.2) | collective-permute-done | bytes 135200 | tf_op jit(solution)/shard_map/ppermute | solution.py:23
  23.8 0.6 %collective-permute-start.3 = (f32[8,64,128]{2,1,0:T(8,128)S(1)}, f32[8,64,128]{2,1,0:T(8,128)S(1)}, u32[]{:S(2)}, u32[]{:S(2)}) collective-permute-start(f32[8,64,128]{2,1,0:T(8,128)S(1)} %get-tuple-element.36.refs_0_), channel_id=1, source_target_pairs={{0,8},{8,0},{16,24},{24,16},{1,9},{9,1},{17,25},{25,17},{2,10},{10... | collective-permute-start | bytes 786440 | tf_op jit(solution)/shard_map/ppermute | solution.py:23
  24.5 1.5 %collective-permute-start.4 = (f32[8,64,128]{2,1,0:T(8,128)S(1)}, f32[8,64,128]{2,1,0:T(8,128)S(1)}, u32[]{:S(2)}, u32[]{:S(2)}) collective-permute-start(f32[8,64,128]{2,1,0:T(8,128)S(1)} %get-tuple-element.36.refs_0_), channel_id=1, source_target_pairs={{0,16},{8,24},{16,0},{24,8},{1,17},{9,25},{17,1},{25,9},{2,18},{10... | collective-permute-start | bytes 786440 | tf_op jit(solution)/shard_map/ppermute | solution.py:23
  26.0 1.4 %collective-permute-start.5 = (f32[8,64,128]{2,1,0:T(8,128)S(1)}, f32[8,64,128]{2,1,0:T(8,128)S(1)}, u32[]{:S(2)}, u32[]{:S(2)}) collective-permute-start(f32[8,64,128]{2,1,0:T(8,128)S(1)} %get-tuple-element.36.refs_0_), channel_id=1, source_target_pairs={{0,24},{8,16},{16,8},{24,0},{1,25},{9,17},{17,9},{25,1},{2,26},{10... | collective-permute-start | bytes 786440 | tf_op jit(solution)/shard_map/ppermute | solution.py:23
  28.1 0.7 %collective-permute-done.11.refs_5_ = f32[4,56,128]{2,1,0:T(8,128)S(1)} collective-permute-done((f32[4,56,128]{2,1,0:T(8,128)S(1)}, f32[4,56,128]{2,1,0:T(8,128)S(1)}, u32[]{:S(2)}, u32[]{:S(2)}) %collective-permute-start.11) | collective-permute-done | bytes 114720 | tf_op jit(solution)/shard_map/ppermute | solution.py:23
  28.8 2.8 %collective-permute-start.17 = (f32[2,4,2,16,128]{4,3,2,1,0:T(8,128)S(1)}, f32[2,4,2,16,128]{4,3,2,1,0:T(8,128)S(1)}, u32[]{:S(2)}, u32[]{:S(2)}) collective-permute-start(f32[2,4,2,16,128]{4,3,2,1,0:T(8,128)S(1)} %get-tuple-element.51), channel_id=1, source_target_pairs={{0,4},{1,5},{2,6},{3,7},{4,0},{5,1},{6,2},{7,3},{8,12},{9,13},{10,... | collective-permute-start | bytes 393224 | tf_op jit(solution)/shard_map/ppermute | solution.py:23
  31.6 4.6 %shard_map.108 = (f32[4,40,128]{2,1,0:T(8,128)S(1)}, f32[4,40,128]{2,1,0:T(8,128)S(1)}, f32[4,40,128]{2,1,0:T(8,128)S(1)}, f32[4,40,128]{2,1,0:T(8,128)S(1)}) custom-call(s32[1]{0:T(128)S(6)} %copy.11.cells, f32[1,8]{1,0:T(1,128)} %traces.3, f32[16,56,128]{2,1,0:T(8,128)S(1)} %get-tuple-element.37.whole, f32[12,56,128]{2,1,0:T(8,128)S(1)} %collective-permute-done.6.refs_0_, ...), custom_call_target="tpu_custom_call" | custom-call | flops 36700160 | bytes 2162720 | tf_op jit(solution)/shard_map/pallas_call | solution.py:43
  36.2 0.6 collective-permute-start.19
  36.8 1.5 %collective-permute-start.20 = (f32[4,40,128]{2,1,0:T(8,128)S(1)}, f32[4,40,128]{2,1,0:T(8,128)S(1)}, u32[]{:S(2)}, u32[]{:S(2)}) collective-permute-start(f32[4,40,128]{2,1,0:T(8,128)S(1)} %get-tuple-element.43), channel_id=1, source_target_pairs={{0,16},{8,24},{16,0},{24,8},{1,17},{9,25},{17,1},{25,9},{2,18},{10... | collective-permute-start | bytes 245768 | tf_op jit(solution)/shard_map/ppermute | solution.py:23
  39.1 1.6 %collective-permute-done.19.refs_1_ = f32[4,40,128]{2,1,0:T(8,128)S(1)} collective-permute-done((f32[4,40,128]{2,1,0:T(8,128)S(1)}, f32[4,40,128]{2,1,0:T(8,128)S(1)}, u32[]{:S(2)}, u32[]{:S(2)}) %collective-permute-start.19) | collective-permute-done | bytes 81952 | tf_op jit(solution)/shard_map/ppermute | solution.py:23
  41.2 2.4 %collective-permute-start.21 = (f32[4,40,128]{2,1,0:T(8,128)S(1)}, f32[4,40,128]{2,1,0:T(8,128)S(1)}, u32[]{:S(2)}, u32[]{:S(2)}) collective-permute-start(f32[4,40,128]{2,1,0:T(8,128)S(1)} %get-tuple-element.44), channel_id=1, source_target_pairs={{0,24},{8,16},{16,8},{24,0},{1,25},{9,17},{17,9},{25,1},{2,26},{10... | collective-permute-start | bytes 245768 | tf_op jit(solution)/shard_map/ppermute | solution.py:23
  43.7 2.9 %collective-permute-done.21.refs_3_ = f32[4,40,128]{2,1,0:T(8,128)S(1)} collective-permute-done((f32[4,40,128]{2,1,0:T(8,128)S(1)}, f32[4,40,128]{2,1,0:T(8,128)S(1)}, u32[]{:S(2)}, u32[]{:S(2)}) %collective-permute-start.21) | collective-permute-done | bytes 81952 | tf_op jit(solution)/shard_map/ppermute | solution.py:23
  46.6 1.7 %collective-permute-start.18 = (f32[4,4,1,16,128]{4,3,2,1,0:T(8,128)S(1)}, f32[4,4,1,16,128]{4,3,2,1,0:T(8,128)S(1)}, u32[]{:S(2)}, u32[]{:S(2)}) collective-permute-start(f32[4,4,1,16,128]{4,3,2,1,0:T(8,128)S(1)} %get-tuple-element.53), channel_id=1, source_target_pairs={{0,2},{1,3},{2,0},{3,1},{4,6},{5,7},{6,4},{7,5},{8,10},{9,11},{10,... | collective-permute-start | bytes 393224 | tf_op jit(solution)/shard_map/ppermute | solution.py:23
  48.3 0.7 %shard_map.112 = f32[4,128,128]{2,1,0:T(8,128)} custom-call(f32[4,40,128]{2,1,0:T(8,128)S(1)} %get-tuple-element.41.refs_0_, f32[4,40,128]{2,1,0:T(8,128)S(1)} %collective-permute-done.19.refs_1_, f32[4,40,128]{2,1,0:T(8,128)S(1)} %collective-permute-done.20.refs_2_, f32[4,40,128]{2,1,0:T(8,128)S(1)} %collective-permute-done.21.refs_3_), custom_call_target="tpu_custom_call" | custom-call | bytes 589824 | tf_op jit(solution)/shard_map/pallas_call | solution.py:43
  49.0 2.5 %collective-permute-done.18.refs_9_ = f32[4,4,1,16,128]{4,3,2,1,0:T(8,128)S(1)} collective-permute-done((f32[4,4,1,16,128]{4,3,2,1,0:T(8,128)S(1)}, f32[4,4,1,16,128]{4,3,2,1,0:T(8,128)S(1)}, u32[]{:S(2)}, u32[]{:S(2)}) %collective-permute-start.18) | collective-permute-done | bytes 131104 | tf_op jit(solution)/shard_map/ppermute | solution.py:23
  51.6 4.8 %shard_map.111 = f32[4,16,128]{2,1,0:T(8,128)} custom-call(s32[8]{0:T(128)} %order.1, f32[8,128]{1,0:T(8,128)S(1)} %get-tuple-element.35.infos, f32[8,64,128]{2,1,0:T(8,128)S(1)} %get-tuple-element.36.refs_0_, f32[8,64,128]{2,1,0:T(8,128)S(1)} %collective-permute-done.3.refs_1_, f32[8,64,128]{2,1,0:T(8,128)S(1)} %collective-permute-done.4.refs_2_, ...), custom_call_target="tpu_custom_call" | custom-call | flops 31457280 | bytes 2396192 | tf_op jit(solution)/shard_map/pallas_call | solution.py:43
  (32 shorter events, 2.7 us)
Async XLA Ops:
  3.4 4.6 %collective-permute-start = (f32[520,128]{1,0:T(8,128)S(1)}, f32[520,128]{1,0:T(8,128)S(1)}, u32[]{:S(2)}, u32[]{:S(2)}) collective-permute-start(f32[520,128]{1,0:T(8,128)S(1)} %get-tuple-element.30.sent), channel_id=1, source_target_pairs={{0,1},{1,0},{2,3},{3,2},{4,5},{5,4},{6,7},{7,6},{8,9},{9,8},{10,11... | collective-permute-start | bytes 798728 | tf_op jit(solution)/shard_map/ppermute | solution.py:23
  3.9 18.6 %collective-permute-start.7 = (f32[12,56,128]{2,1,0:T(8,128)S(1)}, f32[12,56,128]{2,1,0:T(8,128)S(1)}, u32[]{:S(2)}, u32[]{:S(2)}) collective-permute-start(f32[12,56,128]{2,1,0:T(8,128)S(1)} %get-tuple-element.39), channel_id=1, source_target_pairs={{0,16},{8,24},{16,0},{24,8},{1,17},{9,25},{17,1},{25,9},{2,18},{10... | collective-permute-start | bytes 1032200 | tf_op jit(solution)/shard_map/ppermute | solution.py:23
  6.5 19.5 %collective-permute-start.8 = (f32[12,56,128]{2,1,0:T(8,128)S(1)}, f32[12,56,128]{2,1,0:T(8,128)S(1)}, u32[]{:S(2)}, u32[]{:S(2)}) collective-permute-start(f32[12,56,128]{2,1,0:T(8,128)S(1)} %get-tuple-element.40), channel_id=1, source_target_pairs={{0,24},{8,16},{16,8},{24,0},{1,25},{9,17},{17,9},{25,1},{2,26},{10... | collective-permute-start | bytes 1032200 | tf_op jit(solution)/shard_map/ppermute | solution.py:23
  8.0 10.6 %collective-permute-start.1 = (f32[328,128]{1,0:T(8,128)S(1)}, f32[328,128]{1,0:T(8,128)S(1)}, u32[]{:S(2)}, u32[]{:S(2)}) collective-permute-start(f32[328,128]{1,0:T(8,128)S(1)} %get-tuple-element.32), channel_id=1, source_target_pairs={{0,4},{1,5},{2,6},{3,7},{4,0},{5,1},{6,2},{7,3},{8,12},{9,13},{10,... | collective-permute-start | bytes 503816 | tf_op jit(solution)/shard_map/ppermute | solution.py:23
  10.7 16.7 %collective-permute-start.6 = (f32[12,56,128]{2,1,0:T(8,128)S(1)}, f32[12,56,128]{2,1,0:T(8,128)S(1)}, u32[]{:S(2)}, u32[]{:S(2)}) collective-permute-start(f32[12,56,128]{2,1,0:T(8,128)S(1)} %get-tuple-element.38), channel_id=1, source_target_pairs={{0,8},{8,0},{16,24},{24,16},{1,9},{9,1},{17,25},{25,17},{2,10},{10... | collective-permute-start | bytes 1032200 | tf_op jit(solution)/shard_map/ppermute | solution.py:23
  18.7 5.1 %collective-permute-start.2 = (f32[264,128]{1,0:T(8,128)S(1)}, f32[264,128]{1,0:T(8,128)S(1)}, u32[]{:S(2)}, u32[]{:S(2)}) collective-permute-start(f32[264,128]{1,0:T(8,128)S(1)} %get-tuple-element.34), channel_id=1, source_target_pairs={{0,2},{1,3},{2,0},{3,1},{4,6},{5,7},{6,4},{7,5},{8,10},{9,11},{10,... | collective-permute-start | bytes 405512 | tf_op jit(solution)/shard_map/ppermute | solution.py:23
  19.4 5.0 %collective-permute-start.16 = (f32[4,4,16,128]{3,2,1,0:T(8,128)S(1)}, f32[4,4,16,128]{3,2,1,0:T(8,128)S(1)}, u32[]{:S(2)}, u32[]{:S(2)}) collective-permute-start(f32[4,4,16,128]{3,2,1,0:T(8,128)S(1)} %get-tuple-element.49), channel_id=1, source_target_pairs={{0,1},{1,0},{2,3},{3,2},{4,5},{5,4},{6,7},{7,6},{8,9},{9,8},{10,11... | collective-permute-start | bytes 393224 | tf_op jit(solution)/shard_map/ppermute | solution.py:23
  22.5 4.9 %collective-permute-start.10 = (f32[4,56,128]{2,1,0:T(8,128)S(1)}, f32[4,56,128]{2,1,0:T(8,128)S(1)}, u32[]{:S(2)}, u32[]{:S(2)}) collective-permute-start(f32[4,56,128]{2,1,0:T(8,128)S(1)} %slice.13), channel_id=1, source_target_pairs={{0,1},{1,0},{2,3},{3,2},{4,5},{5,4},{6,7},{7,6},{8,9},{9,8},{10,11... | collective-permute-start | bytes 344072 | tf_op jit(solution)/shard_map/ppermute | solution.py:23
  23.8 13.0 %collective-permute-start.3 = (f32[8,64,128]{2,1,0:T(8,128)S(1)}, f32[8,64,128]{2,1,0:T(8,128)S(1)}, u32[]{:S(2)}, u32[]{:S(2)}) collective-permute-start(f32[8,64,128]{2,1,0:T(8,128)S(1)} %get-tuple-element.36.refs_0_), channel_id=1, source_target_pairs={{0,8},{8,0},{16,24},{24,16},{1,9},{9,1},{17,25},{25,17},{2,10},{10... | collective-permute-start | bytes 786440 | tf_op jit(solution)/shard_map/ppermute | solution.py:23
  24.5 14.0 %collective-permute-start.4 = (f32[8,64,128]{2,1,0:T(8,128)S(1)}, f32[8,64,128]{2,1,0:T(8,128)S(1)}, u32[]{:S(2)}, u32[]{:S(2)}) collective-permute-start(f32[8,64,128]{2,1,0:T(8,128)S(1)} %get-tuple-element.36.refs_0_), channel_id=1, source_target_pairs={{0,16},{8,24},{16,0},{24,8},{1,17},{9,25},{17,1},{25,9},{2,18},{10... | collective-permute-start | bytes 786440 | tf_op jit(solution)/shard_map/ppermute | solution.py:23
  26.0 12.5 %collective-permute-start.5 = (f32[8,64,128]{2,1,0:T(8,128)S(1)}, f32[8,64,128]{2,1,0:T(8,128)S(1)}, u32[]{:S(2)}, u32[]{:S(2)}) collective-permute-start(f32[8,64,128]{2,1,0:T(8,128)S(1)} %get-tuple-element.36.refs_0_), channel_id=1, source_target_pairs={{0,24},{8,16},{16,8},{24,0},{1,25},{9,17},{17,9},{25,1},{2,26},{10... | collective-permute-start | bytes 786440 | tf_op jit(solution)/shard_map/ppermute | solution.py:23
  27.4 1.4 %collective-permute-start.11 = (f32[4,56,128]{2,1,0:T(8,128)S(1)}, f32[4,56,128]{2,1,0:T(8,128)S(1)}, u32[]{:S(2)}, u32[]{:S(2)}) collective-permute-start(f32[4,56,128]{2,1,0:T(8,128)S(1)} %slice.14), channel_id=1, source_target_pairs={{0,1},{1,0},{2,3},{3,2},{4,5},{5,4},{6,7},{7,6},{8,9},{9,8},{10,11... | collective-permute-start | bytes 344072 | tf_op jit(solution)/shard_map/ppermute | solution.py:23
  27.5 4.1 %collective-permute-start.9 = (f32[4,56,128]{2,1,0:T(8,128)S(1)}, f32[4,56,128]{2,1,0:T(8,128)S(1)}, u32[]{:S(2)}, u32[]{:S(2)}) collective-permute-start(f32[4,56,128]{2,1,0:T(8,128)S(1)} %slice.12), channel_id=1, source_target_pairs={{0,1},{1,0},{2,3},{3,2},{4,5},{5,4},{6,7},{7,6},{8,9},{9,8},{10,11... | collective-permute-start | bytes 344072 | tf_op jit(solution)/shard_map/ppermute | solution.py:23
  28.8 10.2 %collective-permute-start.17 = (f32[2,4,2,16,128]{4,3,2,1,0:T(8,128)S(1)}, f32[2,4,2,16,128]{4,3,2,1,0:T(8,128)S(1)}, u32[]{:S(2)}, u32[]{:S(2)}) collective-permute-start(f32[2,4,2,16,128]{4,3,2,1,0:T(8,128)S(1)} %get-tuple-element.51), channel_id=1, source_target_pairs={{0,4},{1,5},{2,6},{3,7},{4,0},{5,1},{6,2},{7,3},{8,12},{9,13},{10,... | collective-permute-start | bytes 393224 | tf_op jit(solution)/shard_map/ppermute | solution.py:23
  36.2 4.5 %collective-permute-start.19 = (f32[4,40,128]{2,1,0:T(8,128)S(1)}, f32[4,40,128]{2,1,0:T(8,128)S(1)}, u32[]{:S(2)}, u32[]{:S(2)}) collective-permute-start(f32[4,40,128]{2,1,0:T(8,128)S(1)} %get-tuple-element.42), channel_id=1, source_target_pairs={{0,8},{8,0},{16,24},{24,16},{1,9},{9,1},{17,25},{25,17},{2,10},{10... | collective-permute-start | bytes 245768 | tf_op jit(solution)/shard_map/ppermute | solution.py:23
  36.8 4.4 %collective-permute-start.20 = (f32[4,40,128]{2,1,0:T(8,128)S(1)}, f32[4,40,128]{2,1,0:T(8,128)S(1)}, u32[]{:S(2)}, u32[]{:S(2)}) collective-permute-start(f32[4,40,128]{2,1,0:T(8,128)S(1)} %get-tuple-element.43), channel_id=1, source_target_pairs={{0,16},{8,24},{16,0},{24,8},{1,17},{9,25},{17,1},{25,9},{2,18},{10... | collective-permute-start | bytes 245768 | tf_op jit(solution)/shard_map/ppermute | solution.py:23
  38.5 13.0 %collective-permute-start.12 = (f32[8,64,128]{2,1,0:T(8,128)S(1)}, f32[8,64,128]{2,1,0:T(8,128)S(1)}, u32[]{:S(2)}, u32[]{:S(2)}) collective-permute-start(f32[8,64,128]{2,1,0:T(8,128)S(1)} %get-tuple-element.36.refs_0_), channel_id=1, source_target_pairs={{0,1},{1,0},{2,3},{3,2},{4,5},{5,4},{6,7},{7,6},{8,9},{9,8},{10,11... | collective-permute-start | bytes 786440 | tf_op jit(solution)/shard_map/ppermute | solution.py:23
  38.5 13.0 %collective-permute-start.13 = (f32[8,64,128]{2,1,0:T(8,128)S(1)}, f32[8,64,128]{2,1,0:T(8,128)S(1)}, u32[]{:S(2)}, u32[]{:S(2)}) collective-permute-start(f32[8,64,128]{2,1,0:T(8,128)S(1)} %collective-permute-done.3.refs_1_), channel_id=1, source_target_pairs={{0,1},{1,0},{2,3},{3,2},{4,5},{5,4},{6,7},{7,6},{8,9},{9,8},{10,11... | collective-permute-start | bytes 786440 | tf_op jit(solution)/shard_map/ppermute | solution.py:23
  39.0 12.5 %collective-permute-start.14 = (f32[8,64,128]{2,1,0:T(8,128)S(1)}, f32[8,64,128]{2,1,0:T(8,128)S(1)}, u32[]{:S(2)}, u32[]{:S(2)}) collective-permute-start(f32[8,64,128]{2,1,0:T(8,128)S(1)} %collective-permute-done.4.refs_2_), channel_id=1, source_target_pairs={{0,1},{1,0},{2,3},{3,2},{4,5},{5,4},{6,7},{7,6},{8,9},{9,8},{10,11... | collective-permute-start | bytes 786440 | tf_op jit(solution)/shard_map/ppermute | solution.py:23
  40.7 10.8 %collective-permute-start.15 = (f32[8,64,128]{2,1,0:T(8,128)S(1)}, f32[8,64,128]{2,1,0:T(8,128)S(1)}, u32[]{:S(2)}, u32[]{:S(2)}) collective-permute-start(f32[8,64,128]{2,1,0:T(8,128)S(1)} %collective-permute-done.5.refs_3_), channel_id=1, source_target_pairs={{0,1},{1,0},{2,3},{3,2},{4,5},{5,4},{6,7},{7,6},{8,9},{9,8},{10,11... | collective-permute-start | bytes 786440 | tf_op jit(solution)/shard_map/ppermute | solution.py:23
  41.2 5.3 %collective-permute-start.21 = (f32[4,40,128]{2,1,0:T(8,128)S(1)}, f32[4,40,128]{2,1,0:T(8,128)S(1)}, u32[]{:S(2)}, u32[]{:S(2)}) collective-permute-start(f32[4,40,128]{2,1,0:T(8,128)S(1)} %get-tuple-element.44), channel_id=1, source_target_pairs={{0,24},{8,16},{16,8},{24,0},{1,25},{9,17},{17,9},{25,1},{2,26},{10... | collective-permute-start | bytes 245768 | tf_op jit(solution)/shard_map/ppermute | solution.py:23
  46.6 5.0 %collective-permute-start.18 = (f32[4,4,1,16,128]{4,3,2,1,0:T(8,128)S(1)}, f32[4,4,1,16,128]{4,3,2,1,0:T(8,128)S(1)}, u32[]{:S(2)}, u32[]{:S(2)}) collective-permute-start(f32[4,4,1,16,128]{4,3,2,1,0:T(8,128)S(1)} %get-tuple-element.53), channel_id=1, source_target_pairs={{0,2},{1,3},{2,0},{3,1},{4,6},{5,7},{6,4},{7,5},{8,10},{9,11},{10,... | collective-permute-start | bytes 393224 | tf_op jit(solution)/shard_map/ppermute | solution.py:23
